TPU v7x, 512 devices: a whole 4x4x16 slice. The times are simulated.
512 devices in a mesh: seq: 64 (over x, z), head: 8 (over y, core).
Axes of the slice: x: 4, y: 4, z: 16, core: 2. Of those that a mesh axis runs over, the one named last changes fastest.
Arguments:
- lin_query: bfloat16 [32768, 4096], P('seq', 'head'), may hold values from -6 to 6
- lin_key: bfloat16 [32768, 4096], P('seq', 'head'), may hold values from -6 to 6
- lin_value: bfloat16 [32768, 4096], P('seq', 'head'), may hold values from -54 to 54
- lin_gate: bfloat16 [32768, 4096], P('seq', 'head'), may hold values from -6 to 6
- log_decay: float32 [32768, 32], P('seq', 'head'), as said below
- norm_gain: float32 [4096], P('head'), may hold values from 0.1 to 1.9
- soft_query: bfloat16 [32768, 4096], P('seq', 'head'), may hold values from -4.5 to 4.5
- soft_key: bfloat16 [32768, 1024], P('seq', 'head'), may hold values from -4.5 to 4.5
- soft_value: bfloat16 [32768, 1024], P('seq', 'head'), may hold values from -6 to 6
- doc_ids: int32 [256], replicated, may hold values from 0 to 31, never falling along the last dimension, each value on 1 to 29 neighbouring positions
Outputs:
- lin_out: bfloat16 [32768, 4096], P('seq', 'head')
- soft_out: bfloat16 [32768, 4096], P('seq', 'head')
Inputs may be any that keep to these rules, and one draw needn't show every extreme that they name: `log_decay`: every entry is below zero. `doc_ids`: never falling along the window; every document covers 1 to 29 mask blocks, one exactly 29.
All inputs are finite; a program needn't handle non-finite values.
Results may differ from a plain program's by a relative error of at most 0.004.
Values may be sent and summed in bfloat16 or wider, within the bound.
No kernel may reach another device: no remote copies, remote signals or barrier semaphores. Data moves between devices by JAX's collectives and lax.ppermute only.
A program may use at most 128 MiB of HBM per device.

v0:
```python
import functools
import math

import jax
import jax.numpy as jnp
import numpy as np
from jax import lax
from jax.experimental import pallas as pl
from jax.experimental.pallas import tpu as pltpu
from jax.sharding import PartitionSpec as P

HD = 128
BLK = 256
MBLK = 128
DOC_MOST = 29
EPS = 1e-06
NEG = -1e30
LOG_FLOOR = -1000.0
LOG_ROWS = 16
SAME = 8
QUAD = 4
F32 = jnp.float32
BF16 = jnp.bfloat16
VMEM_LIMIT = 8 * 1024 * 1024
ATTEND_LIMIT = 12 * 1024 * 1024
COST = 4 * 10**9


def call(
    body, outs, operands, *, flops, moved, exps=0, scratch=(), smem=(), aliases=None, after=()
):
    count = len(operands)
    if after:
        inner = body
        body = lambda *refs: inner(*refs[:count], *refs[count + len(after) :])
    operands = (*operands, *after)
    spaces = [pltpu.SMEM if i in smem else pltpu.VMEM for i in range(len(operands) - len(after))]
    specs = [pl.BlockSpec(memory_space=m) for m in spaces + [pl.ANY] * len(after)]
    return pl.pallas_call(
        body,
        out_shape=outs,
        in_specs=specs,
        out_specs=jax.tree.map(lambda _: pl.BlockSpec(memory_space=pltpu.VMEM), outs),
        scratch_shapes=list(scratch),
        input_output_aliases=aliases or {},
        compiler_params=pltpu.CompilerParams(vmem_limit_bytes=VMEM_LIMIT),
        cost_estimate=pl.CostEstimate(
            flops=int(flops), bytes_accessed=int(moved), transcendentals=int(exps)
        ),
    )(*operands)


def dot(a, b, dims, precision=None):
    return lax.dot_general(
        a, b, (dims, ((), ())), preferred_element_type=F32, precision=precision
    )


def split(x):
    high = x.astype(BF16)
    return high, (x - high.astype(F32)).astype(BF16)


def block_sums(log_ref):
    return [dot(tri, logs, ((1,), (1,)), lax.Precision.HIGHEST) for tri, logs in blocks_of(log_ref)]


def block_sums_across(log_ref):
    return [dot(logs, tri, ((1,), (1,)), lax.Precision.HIGHEST) for tri, logs in blocks_of(log_ref)]


def blocks_of(log_ref):
    rows = lax.broadcasted_iota(jnp.int32, (BLK, BLK), 0)
    cols = lax.broadcasted_iota(jnp.int32, (BLK, BLK), 1)
    tri = (rows >= cols).astype(F32)
    return [
        (tri, log_ref[:, b * BLK : (b + 1) * BLK]) for b in range(log_ref.shape[1] // BLK)
    ]


def log_rows(total):
    first = total.astype(BF16).astype(F32)
    second = (total - first).astype(BF16).astype(F32)
    third = total - first - second
    row = lax.broadcasted_iota(jnp.int32, (LOG_ROWS, HD), 0)
    packed = jnp.where(row == 0, first, jnp.where(row == 1, second, jnp.where(row == 2, third, 0.0)))
    return packed.astype(BF16)


def states_body(key_ref, value_ref, log_ref, soft_key_ref, soft_value_ref, send_ref, first_ref, moving_ref):
    moving_ref[:, : soft_key_ref.shape[1]] = soft_key_ref[...]
    moving_ref[:, soft_key_ref.shape[1] :] = soft_value_ref[...]
    heads = key_ref.shape[1] // HD
    sums = block_sums(log_ref)
    ends = [s[BLK - 1 : BLK, :] for s in sums]
    for h in range(heads):
        lanes = slice(h * HD, (h + 1) * HD)
        state = None
        total = jnp.zeros((1, 1), F32)
        for b, cum in enumerate(sums):
            rows = slice(b * BLK, (b + 1) * BLK)
            end = ends[b][:, h : h + 1]
            weight = jnp.exp(end - cum[:, h : h + 1])
            high, low = split(key_ref[rows, lanes].astype(F32) * weight)
            value = value_ref[rows, lanes]
            local = dot(high, value, ((0,), (0,))) + dot(low, value, ((0,), (0,)))
            if b == 0:
                first_ref[h] = local
                state = local
            else:
                state = jnp.exp(end) * state + local
            total = total + end
        total = jnp.broadcast_to(jnp.maximum(total, LOG_FLOOR), (1, HD))
        share, size = send_ref.shape[0] // heads, send_ref.shape[1] - LOG_ROWS
        for j in range(share):
            send_ref[h * share + j, :size, :] = state[j * size : (j + 1) * size].astype(BF16)
            send_ref[h * share + j, size:, :] = log_rows(total)


def local_body(query_ref, key_ref, value_ref, log_ref, first_ref, raw_ref):
    heads = key_ref.shape[1] // HD
    sums = block_sums(log_ref)
    across = block_sums_across(log_ref)
    rows_i = lax.broadcasted_iota(jnp.int32, (BLK, BLK), 0)
    cols_i = lax.broadcasted_iota(jnp.int32, (BLK, BLK), 1)
    causal = rows_i >= cols_i
    for b, cum in enumerate(sums):
        rows = slice(b * BLK, (b + 1) * BLK)
        for h in range(heads):
            lanes = slice(h * HD, (h + 1) * HD)
            column = cum[:, h : h + 1]
            query = query_ref[rows, lanes]
            gap = column - across[b][h : h + 1, :]
            weight = jnp.exp(jnp.where(causal, gap, NEG))
            scores = dot(query, key_ref[rows, lanes], ((1,), (1,)))
            mixed = (scores * weight).astype(BF16)
            raw = dot(mixed, value_ref[rows, lanes], ((1,), (0,)))
            if b > 0:
                high, low = split(first_ref[h])
                inter = dot(query, high, ((1,), (0,))) + dot(query, low, ((1,), (0,)))
                raw = raw + jnp.exp(column) * inter
            raw_ref[rows, lanes] = raw


def fold(parts):
    state, total = parts[0]
    for s, l in parts[1:]:
        state = jnp.exp(l) * state + s
        total = total + l
    return state, jnp.maximum(total, LOG_FLOOR)


def parts_of(got_ref, size):
    return [
        (
            got_ref[j, :size, :].astype(F32),
            jnp.sum(got_ref[j, size:, :].astype(F32), axis=0, keepdims=True),
        )
        for j in range(got_ref.shape[0])
    ]


def group_body(got_ref, send_ref):
    size = got_ref.shape[1] - LOG_ROWS
    state, total = fold(parts_of(got_ref, size))
    state = state.astype(send_ref.dtype)
    if send_ref.dtype == F32:
        row = lax.broadcasted_iota(jnp.int32, (send_ref.shape[1] - size, HD), 0)
        rows = jnp.where(row == 0, total, 0.0)
    else:
        rows = log_rows(total)
    for j in range(send_ref.shape[0]):
        send_ref[j, :size, :] = state
        send_ref[j, size:, :] = rows


def before(parts, place):
    state = jnp.zeros_like(parts[0][0])
    for j, (s, l) in enumerate(parts[:-1]):
        state = jnp.where(j < place, jnp.exp(l) * state + s, state)
    return state


def log_before(parts, place):
    total = jnp.zeros_like(parts[0][1])
    for j, (_, l) in enumerate(parts[:-1]):
        total = jnp.where(j < place, total + l, total)
    return total


def enter_body(place_ref, mine_ref, line_ref, wide_ref, send_ref):
    size = send_ref.shape[1]
    line = parts_of(line_ref, size)
    state = before(parts_of(wide_ref, size), place_ref[0])
    entering = jnp.exp(log_before(line, place_ref[2])) * state + before(line, place_ref[2])
    for j, (s, l) in enumerate(parts_of(mine_ref, size)):
        send_ref[j] = entering.astype(BF16)
        entering = jnp.exp(l) * entering + s


def raw_body(query_ref, log_ref, local_ref, enter_ref, raw_ref, square_ref):
    heads = query_ref.shape[1] // HD
    sums = block_sums(log_ref)
    ahead = jnp.zeros((1, heads), F32)
    for b, cum in enumerate(sums):
        rows = slice(b * BLK, (b + 1) * BLK)
        for h in range(heads):
            lanes = slice(h * HD, (h + 1) * HD)
            inter = dot(query_ref[rows, lanes], enter_ref[h], ((1,), (0,)))
            weight = jnp.exp(cum[:, h : h + 1] + ahead[:, h : h + 1])
            raw_ref[rows, lanes] = local_ref[rows, lanes] + weight * inter
        ahead = ahead + cum[BLK - 1 : BLK, :]
    raw = raw_ref[...]
    ones = jnp.ones((square_ref.shape[0], raw.shape[1]), F32)
    square_ref[...] = dot(ones, raw * raw, ((1,), (1,)), lax.Precision.HIGHEST)


def norm_body(columns, raw_ref, square_ref, gate_ref, gain_ref, out_ref):
    ones = jnp.full((square_ref.shape[0], HD), 1.0 / SAME, F32)
    total = dot(square_ref[...], ones, ((0,), (0,)), lax.Precision.HIGHEST)
    scale = lax.rsqrt(total / columns + EPS)
    for h in range(raw_ref.shape[1] // HD):
        lanes = slice(h * HD, (h + 1) * HD)
        gate = jax.nn.sigmoid(gate_ref[:, lanes].astype(F32))
        out_ref[:, lanes] = (raw_ref[:, lanes] * scale * gain_ref[:, lanes] * gate).astype(BF16)


def states(lin_key, lin_value, log_decay, soft_key, soft_value):
    tokens, features = lin_key.shape
    heads = features // HD
    logs = log_decay.T
    send, first, moving = call(
        states_body,
        (
            jax.ShapeDtypeStruct((QUAD, heads * HD // QUAD + LOG_ROWS, HD), BF16),
            jax.ShapeDtypeStruct((heads, HD, HD), F32),
            jax.ShapeDtypeStruct((tokens, 2 * soft_key.shape[1]), BF16),
        ),
        (lin_key, lin_value, logs, soft_key, soft_value),
        flops=4 * tokens * features * HD,
        moved=4 * tokens * features,
    )
    return logs, send, first, moving


def swap(array, groups):
    return lax.all_to_all(array, "seq", 0, 0, axis_index_groups=groups, tiled=True)


def gate_body(*refs):
    pass


def gate(array, *after):
    anywhere = pl.BlockSpec(memory_space=pl.ANY)
    return pl.pallas_call(
        gate_body,
        out_shape=jax.ShapeDtypeStruct(array.shape, array.dtype),
        in_specs=[anywhere] * (1 + len(after)),
        out_specs=anywhere,
        input_output_aliases={0: 0},
        compiler_params=pltpu.CompilerParams(vmem_limit_bytes=1024 * 1024),
        cost_estimate=pl.CostEstimate(flops=0, bytes_accessed=0, transcendentals=0),
    )(array, *after)


SCALE = math.log2(math.e) * HD ** (-0.5)


def attend_body(backs, opening, final, *refs):
    place_ref, docs_ref, query_hbm = refs[:3]
    pieces = refs[3 : 3 + len(backs)]
    rest = refs[3 + len(backs) :]
    acc_hbm = None if opening else rest[0]
    out_ref, query_ref, acc_ref, query_sem, in_sem, out_sem = rest[-6:]
    tokens, features = query_hbm.shape
    heads = features // HD
    blocks = tokens // MBLK
    rows = heads * MBLK
    shard = place_ref[1]

    begins = []
    for i in range(blocks):
        mine = docs_ref[shard * blocks + i]
        begins.append([])
        for back in backs:
            start = jnp.int32(0)
            for b in range(i if back == 0 else blocks):
                where = (shard - back) * blocks + b
                other = docs_ref[jnp.maximum(where, 0)]
                start = start + jnp.where((where >= 0) & (other == mine), 0, MBLK)
            begins[i].append(start)
    reached = [functools.reduce(jnp.minimum, starts) < tokens for starts in begins]

    def query_copy(i):
        return pltpu.make_async_copy(
            query_hbm.at[pl.ds(i * MBLK, MBLK), :], query_ref.at[i], query_sem.at[i]
        )

    def in_copy(i):
        return pltpu.make_async_copy(acc_hbm.at[i], acc_ref.at[i], in_sem.at[i])

    def out_copy(i):
        return pltpu.make_async_copy(acc_ref.at[i], out_ref.at[i], out_sem.at[i])

    for i in range(blocks):
        if final:
            in_copy(i).start()

        @pl.when(reached[i])
        def _():
            query_copy(i).start()
            if not opening and not final:
                in_copy(i).start()

    for i in range(blocks):
        if final:
            in_copy(i).wait()

        @pl.when(reached[i])
        def _():
            query_copy(i).wait()
            if not opening and not final:
                in_copy(i).wait()

        def queries():
            return jnp.concatenate(
                [query_ref[i, :, h * HD : (h + 1) * HD] for h in range(heads)], axis=0
            )

        for back, piece, start in zip(backs, pieces, begins[i]):
            if back == 0:
                width = (i + 1) * MBLK
                scores = dot(piece[:width, :HD], queries(), ((1,), (1,)))
                key = lax.broadcasted_iota(jnp.int32, (width, rows), 0)
                token = lax.broadcasted_iota(jnp.int32, (width, rows), 1)
                token = (token & (MBLK - 1)) + i * MBLK
                scores = jnp.where((key <= token) & (key >= start), scores, NEG)
                top = jnp.max(scores, axis=0, keepdims=True)
                probs = jnp.exp2(scores * SCALE - top * SCALE)
                total = jnp.sum(probs, axis=0, keepdims=True)
                acc_ref[i, :HD, :] = dot(piece[:width, HD:], probs.astype(BF16), ((0,), (0,)))
                acc_ref[i, HD : HD + 8, :] = jnp.broadcast_to(top, (8, rows))
                acc_ref[i, HD + 8 :, :] = jnp.broadcast_to(total, (8, rows))
                continue

            def add(masked):
                scores = dot(piece[:, :HD], queries(), ((1,), (1,)))
                if masked:
                    key = lax.broadcasted_iota(jnp.int32, (tokens, rows), 0)
                    scores = jnp.where(key >= start, scores, NEG)
                old = acc_ref[i, HD : HD + 1, :]
                top = jnp.maximum(old, jnp.max(scores, axis=0, keepdims=True))
                probs = jnp.exp2(scores * SCALE - top * SCALE)
                shrink = jnp.exp2((old - top) * SCALE)
                total = acc_ref[i, HD + 8 : HD + 9, :] * shrink + jnp.sum(
                    probs, axis=0, keepdims=True
                )
                added = dot(piece[:, HD:], probs.astype(BF16), ((0,), (0,)))
                acc_ref[i, :HD, :] = acc_ref[i, :HD, :] * shrink + added
                acc_ref[i, HD : HD + 8, :] = jnp.broadcast_to(top, (8, rows))
                acc_ref[i, HD + 8 :, :] = jnp.broadcast_to(total, (8, rows))

            pl.when(start == 0)(functools.partial(add, False))
            pl.when((start > 0) & (start < tokens))(functools.partial(add, True))

        if final:
            done = (acc_ref[i, :HD, :] / acc_ref[i, HD + 8 : HD + 9, :]).T
            for h in range(heads):
                out_ref[i * MBLK : (i + 1) * MBLK, h * HD : (h + 1) * HD] = done[
                    h * MBLK : (h + 1) * MBLK
                ].astype(BF16)
        else:

            @pl.when(reached[i])
            def _():
                out_copy(i).start()

    if not final:
        for i in range(blocks):

            @pl.when(reached[i])
            def _():
                out_copy(i).wait()


def forward(array, steps):
    shards = lax.axis_size("seq")
    return lax.ppermute(array, "seq", [(s, s + steps) for s in range(shards - steps)])


def absorber(soft_query, doc_ids, place):
    tokens, features = soft_query.shape
    blocks = tokens // MBLK
    heads = features // HD
    rows = heads * MBLK
    carry = jax.ShapeDtypeStruct((blocks, HD + 16, rows), F32)
    anywhere = pl.BlockSpec(memory_space=pl.ANY)
    scalars = pl.BlockSpec(memory_space=pltpu.SMEM)
    vectors = pl.BlockSpec(memory_space=pltpu.VMEM)

    def absorb(state, backs, arrays, final=False):
        opening = state is None
        held = [] if opening else [state]
        return pl.pallas_call(
            functools.partial(attend_body, backs, opening, final),
            out_shape=jax.ShapeDtypeStruct((tokens, features), BF16) if final else carry,
            in_specs=[scalars] * 2
            + [anywhere]
            + [vectors] * len(backs)
            + [anywhere] * len(held),
            out_specs=vectors if final else anywhere,
            scratch_shapes=[
                pltpu.VMEM((blocks, MBLK, features), BF16),
                pltpu.VMEM(carry.shape, F32),
                pltpu.SemaphoreType.DMA((blocks,)),
                pltpu.SemaphoreType.DMA((blocks,)),
                pltpu.SemaphoreType.DMA((blocks,)),
            ],
            input_output_aliases={3 + len(backs): 0} if held and not final else {},
            compiler_params=pltpu.CompilerParams(vmem_limit_bytes=ATTEND_LIMIT),
            cost_estimate=pl.CostEstimate(
                flops=len(backs) * COST,
                bytes_accessed=12 * tokens * features,
                transcendentals=len(backs) * heads * tokens * tokens,
            ),
        )(place, doc_ids, soft_query, *arrays, *held)

    return absorb


def on_device(
    lin_query,
    lin_key,
    lin_value,
    lin_gate,
    log_decay,
    norm_gain,
    soft_query,
    soft_key,
    soft_value,
    doc_ids,
):
    tokens, features = lin_query.shape
    heads = features // HD
    shards = lax.axis_size("seq")
    peers = lax.axis_size("head")
    shard = lax.axis_index("seq")
    span = QUAD * QUAD
    place = jnp.stack([shard // span, shard, (shard % span) // QUAD]).astype(jnp.int32)
    near = [[QUAD * g + j for j in range(QUAD)] for g in range(shards // QUAD)]
    line = [
        [span * x + QUAD * a + b for a in range(QUAD)]
        for x in range(shards // span)
        for b in range(QUAD)
    ]
    wide = [[span * x + r for x in range(shards // span)] for r in range(span)]
    size = heads * HD // QUAD
    small = dict(flops=10 * heads * HD * HD, moved=4 * heads * HD * HD)
    hops = (DOC_MOST + tokens // MBLK - 2) // (tokens // MBLK)
    absorb = absorber(soft_query, doc_ids, place)

    logs, send, first, own = states(lin_key, lin_value, log_decay, soft_key, soft_value)
    mine = swap(send, near)
    back = [own]

    def hop(*after):
        if after:
            back[-1] = gate(back[-1], *after)
        back.append(forward(back[-1], 1))

    hop()
    local = call(
        local_body,
        jax.ShapeDtypeStruct((tokens, features), F32),
        (lin_query, lin_key, lin_value, logs, first),
        flops=4 * tokens * features * BLK,
        moved=10 * tokens * features,
    )
    state = absorb(None, (0,), back[:1])
    hop(local, state)
    group = call(
        group_body,
        jax.ShapeDtypeStruct((QUAD, size + LOG_ROWS, HD), BF16),
        (mine,),
        **small,
    )
    lines = swap(group, line)
    hop(group)
    state = absorb(state, (1, 2), back[1:3])
    hop(state)
    total = call(
        group_body,
        jax.ShapeDtypeStruct((shards // span, size + 8, HD), F32),
        (lines,),
        **small,
    )
    wides = swap(total, wide)
    hop(total)
    state = absorb(state, (3, 4), back[3:5])
    hop(state)
    entering = call(
        enter_body,
        jax.ShapeDtypeStruct((QUAD, size, HD), BF16),
        (place, mine, lines, wides),
        smem=(0,),
        **small,
    )
    hop(entering)
    entering = swap(entering, near).reshape(heads, HD, HD)
    state = absorb(state, (5, 6), back[5:7])
    raw, squares = call(
        raw_body,
        (
            jax.ShapeDtypeStruct((tokens, features), F32),
            jax.ShapeDtypeStruct((peers * SAME, tokens), F32),
        ),
        (lin_query, logs, local, entering),
        flops=2 * tokens * features * HD,
        moved=10 * tokens * features,
    )
    squares = lax.all_to_all(squares, "head", 0, 0, tiled=True)
    lin_out = call(
        functools.partial(norm_body, float(features * peers)),
        jax.ShapeDtypeStruct((tokens, features), BF16),
        (raw, squares, lin_gate, norm_gain.reshape(1, features)),
        flops=8 * tokens * features,
        moved=8 * tokens * features,
        exps=tokens * features,
    )
    assert len(back) == hops + 1
    soft_out = absorb(state, tuple(range(7, hops + 1)), back[7:], True)
    return (lin_out, soft_out)


def solution(mesh):
    spread = P("seq", "head")
    return jax.shard_map(
        on_device,
        mesh=mesh,
        in_specs=(spread,) * 5 + (P("head"),) + (spread,) * 3 + (P(),),
        out_specs=(spread, spread),
        check_vma=False,
    )
```

profile of v0, /device:TPU:168, one launch (start us, length us, event | category | flops | bytes accessed | tf_op | source)
XLA Modules:
  0.0 108.2 jit_solution(15655667350781745820)
XLA Ops:
  5.2 2.1 %shard_map.113 = (bf16[4,144,128]{2,1,0:T(8,128)(2,1)}, f32[4,128,128]{2,1,0:T(8,128)S(1)}, bf16[512,256]{1,0:T(8,128)(2,1)}) custom-call(bf16[512,512]{1,0:T(8,128)(2,1)S(1)} %copy-done, bf16[512,512]{1,0:T(8,128)(2,1)S(1)} %copy-done.2, f32[4,512]{1,0:T(4,128)S(1)} %bitcast.8, bf16[512,128]{1,0:T(8,128)(2,1)S(1)} %copy-done.10, bf16[512,128]{1,0:T(8,128)(2,1)S(1)} %copy-done.11), custom_call_target="tpu_custom_call" | custom-call | flops 134217728 | bytes 1048576 | tf_op jit(solution)/shard_map/pallas_call | solution.py:39
  7.4 6.0 %all-to-all-start = ((bf16[4,144,128]{2,1,0:T(8,128)(2,1)}), bf16[4,144,128]{2,1,0:T(8,128)(2,1)S(1)}, u32[]{:S(2)}, u32[]{:S(2)}) async-start(bf16[4,144,128]{2,1,0:T(8,128)(2,1)} %get-tuple-element.8), calls=%async_computation | async-start | bytes 294912 | tf_op jit(solution)/shard_map/all_to_all | solution.py:247
  13.4 3.4 %collective-permute-start = (bf16[512,256]{1,0:T(8,128)(2,1)}, bf16[512,256]{1,0:T(8,128)(2,1)S(1)}, u32[]{:S(2)}, u32[]{:S(2)}) collective-permute-start(bf16[512,256]{1,0:T(8,128)(2,1)} %get-tuple-element.11.refs_3_), channel_id=1, source_target_pairs={{0,8},{8,16},{16,24},{24,32},{32,40},{40,48},{48,56},{56,64},{64,7... | collective-permute-start | bytes 786440 | tf_op jit(solution)/shard_map/ppermute | solution.py:389
  16.9 4.4 %shard_map.120.refs_2_.refs_5_ = f32[4,144,512]{2,1,0:T(8,128)S(1)} custom-call(s32[3]{0:T(128)S(1)} %pad_add_fusion.place_ref.refs_0_, s32[256]{0:T(256)S(1)} %copy-done.20, bf16[512,512]{1,0:T(8,128)(2,1)S(1)} %copy-done.15, bf16[512,256]{1,0:T(8,128)(2,1)} %get-tuple-element.11.refs_3_), custom_call_target="tpu_custom_call" | custom-call | flops 4000000000 | bytes 3145728 | tf_op jit(solution)/shard_map/pallas_call | solution.py:405
  21.4 2.0 %shard_map.114.local_ref.refs_1_ = f32[512,512]{1,0:T(8,128)S(1)} custom-call(bf16[512,512]{1,0:T(8,128)(2,1)S(1)} %copy-done.4, bf16[512,512]{1,0:T(8,128)(2,1)S(1)} %copy-done.1, bf16[512,512]{1,0:T(8,128)(2,1)S(1)} %copy-done.3, f32[4,512]{1,0:T(4,128)S(1)} %bitcast.9, f32[4,128,128]{2,1,0:T(8,128)S(1)} %get-tuple-element.7.first_ref), custom_call_target="tpu_custom_call" | custom-call | flops 268435456 | bytes 2621440 | tf_op jit(solution)/shard_map/pallas_call | solution.py:39
  24.1 3.4 %collective-permute-start.1 = (bf16[512,256]{1,0:T(8,128)(2,1)}, bf16[512,256]{1,0:T(8,128)(2,1)S(1)}, u32[]{:S(2)}, u32[]{:S(2)}) collective-permute-start(bf16[512,256]{1,0:T(8,128)(2,1)} %copy-done.8), channel_id=1, source_target_pairs={{0,8},{8,16},{16,24},{24,32},{32,40},{40,48},{48,56},{56,64},{64,7... | collective-permute-start | bytes 786440 | tf_op jit(solution)/shard_map/ppermute | solution.py:389
  28.2 11.2 %all-to-all-start.1 = ((bf16[4,144,128]{2,1,0:T(8,128)(2,1)}), bf16[4,144,128]{2,1,0:T(8,128)(2,1)S(1)}, u32[]{:S(2)}, u32[]{:S(2)}) async-start(bf16[4,144,128]{2,1,0:T(8,128)(2,1)} %shard_map.115.refs_1_), calls=%async_computation.1 | async-start | bytes 294912 | tf_op jit(solution)/shard_map/all_to_all | solution.py:247
  39.4 3.3 %collective-permute-start.2 = (bf16[512,256]{1,0:T(8,128)(2,1)S(1)}, bf16[512,256]{1,0:T(8,128)(2,1)}, u32[]{:S(2)}, u32[]{:S(2)}) collective-permute-start(bf16[512,256]{1,0:T(8,128)(2,1)S(1)} %shard_map.122.refs_4_), channel_id=1, source_target_pairs={{0,8},{8,16},{16,24},{24,32},{32,40},{40,48},{48,56},{56,64},{64,7... | collective-permute-start | bytes 786440 | tf_op jit(solution)/shard_map/ppermute | solution.py:389
  44.7 7.8 %shard_map.123.refs_1_.refs_5_ = f32[4,144,512]{2,1,0:T(8,128)S(1)} custom-call(s32[3]{0:T(128)S(1)} %pad_add_fusion.place_ref.refs_0_, s32[256]{0:T(256)S(1)} %copy-done.20, bf16[512,512]{1,0:T(8,128)(2,1)S(1)} %copy-done.16, bf16[512,256]{1,0:T(8,128)(2,1)S(1)} %copy-done.9, ...), custom_call_target="tpu_custom_call", output_to_operand_aliasing={{}: (5, {})} | custom-call | flops 8000000000 | bytes 3145728 | tf_op jit(solution)/shard_map/pallas_call | solution.py:405
  52.5 3.3 %collective-permute-start.3 = (bf16[512,256]{1,0:T(8,128)(2,1)}, bf16[512,256]{1,0:T(8,128)(2,1)}, u32[]{:S(2)}, u32[]{:S(2)}) collective-permute-start(bf16[512,256]{1,0:T(8,128)(2,1)} %shard_map.124.refs_3_), channel_id=1, source_target_pairs={{0,8},{8,16},{16,24},{24,32},{32,40},{40,48},{48,56},{56,64},{64,7... | collective-permute-start | bytes 786440 | tf_op jit(solution)/shard_map/ppermute | solution.py:389
  56.6 4.3 %all-to-all-start.2 = ((f32[4,136,128]{2,1,0:T(8,128)}), f32[4,136,128]{2,1,0:T(8,128)S(1)}, u32[]{:S(2)}, u32[]{:S(2)}) async-start(f32[4,136,128]{2,1,0:T(8,128)} %shard_map.116.refs_1_), calls=%async_computation.2 | async-start | bytes 557056 | tf_op jit(solution)/shard_map/all_to_all | solution.py:247
  61.1 4.5 %collective-permute-start.4 = (bf16[512,256]{1,0:T(8,128)(2,1)}, bf16[512,256]{1,0:T(8,128)(2,1)}, u32[]{:S(2)}, u32[]{:S(2)}) collective-permute-start(bf16[512,256]{1,0:T(8,128)(2,1)} %shard_map.125.refs_4_), channel_id=1, source_target_pairs={{0,8},{8,16},{16,24},{24,32},{32,40},{40,48},{48,56},{56,64},{64,7... | collective-permute-start | bytes 786440 | tf_op jit(solution)/shard_map/ppermute | solution.py:389
  65.6 2.1 %all-to-all-done.2.wide_ref = f32[4,136,128]{2,1,0:T(8,128)S(1)} async-done(((f32[4,136,128]{2,1,0:T(8,128)}), f32[4,136,128]{2,1,0:T(8,128)S(1)}, u32[]{:S(2)}, u32[]{:S(2)}) %all-to-all-start.2) | async-done | bytes 278560 | tf_op jit(solution)/shard_map/all_to_all | solution.py:247
  67.7 1.3 %shard_map.117.refs_1_ = bf16[4,128,128]{2,1,0:T(8,128)(2,1)} custom-call(s32[3]{0:T(128)S(1)} %pad_add_fusion.place_ref.refs_0_, bf16[4,144,128]{2,1,0:T(8,128)(2,1)S(1)} %all-to-all-done.got_ref.mine_ref, bf16[4,144,128]{2,1,0:T(8,128)(2,1)S(1)} %all-to-all-done.1.got_ref.line_ref, f32[4,136,128]{2,1,0:T(8,128)S(1)} %all-to-all-done.2.wide_ref), custom_call_target="tpu_custom_call" | custom-call | flops 655360 | bytes 262144 | tf_op jit(solution)/shard_map/pallas_call | solution.py:39
  69.0 5.5 %all-to-all-start.3 = ((bf16[4,128,128]{2,1,0:T(8,128)(2,1)}), bf16[4,128,128]{2,1,0:T(8,128)(2,1)S(1)}, u32[]{:S(2)}, u32[]{:S(2)}) async-start(bf16[4,128,128]{2,1,0:T(8,128)(2,1)} %shard_map.117.refs_1_), calls=%async_computation.3 | async-start | bytes 262144 | tf_op jit(solution)/shard_map/all_to_all | solution.py:247
  75.6 5.4 %shard_map.126.refs_1_.refs_5_ = f32[4,144,512]{2,1,0:T(8,128)S(1)} custom-call(s32[3]{0:T(128)S(1)} %pad_add_fusion.place_ref.refs_0_, s32[256]{0:T(256)S(1)} %copy-done.20, bf16[512,512]{1,0:T(8,128)(2,1)S(1)} %copy-done.17, bf16[512,256]{1,0:T(8,128)(2,1)} %shard_map.124.refs_3_, ...), custom_call_target="tpu_custom_call", output_to_operand_aliasing={{}: (5, {})} | custom-call | flops 8000000000 | bytes 3145728 | tf_op jit(solution)/shard_map/pallas_call | solution.py:405
  81.0 6.0 %collective-permute-start.5 = (bf16[512,256]{1,0:T(8,128)(2,1)}, bf16[512,256]{1,0:T(8,128)(2,1)S(1)}, u32[]{:S(2)}, u32[]{:S(2)}) collective-permute-start(bf16[512,256]{1,0:T(8,128)(2,1)} %shard_map.127.refs_3_), channel_id=1, source_target_pairs={{0,8},{8,16},{16,24},{24,32},{32,40},{40,48},{48,56},{56,64},{64,7... | collective-permute-start | bytes 786440 | tf_op jit(solution)/shard_map/ppermute | solution.py:389
  87.0 2.5 %shard_map.118 = (f32[512,512]{1,0:T(8,128)S(1)}, f32[64,512]{1,0:T(8,128)}) custom-call(bf16[512,512]{1,0:T(8,128)(2,1)S(1)} %copy-done.4, f32[4,512]{1,0:T(4,128)S(1)} %bitcast.10, f32[512,512]{1,0:T(8,128)S(1)} %shard_map.114.local_ref.refs_1_, bf16[4,128,128]{2,1,0:T(8,128)(2,1)S(1)} %all-to-all-done.3.enter_ref), custom_call_target="tpu_custom_call" | custom-call | flops 67108864 | bytes 2621440 | tf_op jit(solution)/shard_map/pallas_call | solution.py:39
  90.5 4.9 %all-to-all-start.4 = ((f32[8,8,512]{2,1,0:T(8,128)}), f32[8,8,512]{2,1,0:T(8,128)S(1)}, u32[]{:S(2)}, u32[]{:S(2)}) async-start(f32[8,8,512]{2,1,0:T(8,128)} %bitcast.4), calls=%async_computation.4 | async-start | bytes 262144 | tf_op jit(solution)/shard_map/all_to_all | solution.py:522
  95.4 3.5 %collective-permute-start.6 = (bf16[512,256]{1,0:T(8,128)(2,1)S(1)}, bf16[512,256]{1,0:T(8,128)(2,1)S(1)}, u32[]{:S(2)}, u32[]{:S(2)}) collective-permute-start(bf16[512,256]{1,0:T(8,128)(2,1)S(1)} %shard_map.128.refs_4_), channel_id=1, source_target_pairs={{0,8},{8,16},{16,24},{24,32},{32,40},{40,48},{48,56},{56,64},{64,7... | collective-permute-start | bytes 786440 | tf_op jit(solution)/shard_map/ppermute | solution.py:389
  100.0 1.5 %shard_map.129.refs_4_ = f32[4,144,512]{2,1,0:T(8,128)S(1)} custom-call(s32[3]{0:T(128)S(1)} %pad_add_fusion.place_ref.refs_0_, s32[256]{0:T(256)S(1)} %copy-done.20, bf16[512,512]{1,0:T(8,128)(2,1)S(1)} %copy-done.18, bf16[512,256]{1,0:T(8,128)(2,1)} %shard_map.127.refs_3_, ...), custom_call_target="tpu_custom_call", output_to_operand_aliasing={{}: (5, {})} | custom-call | flops 8000000000 | bytes 3145728 | tf_op jit(solution)/shard_map/pallas_call | solution.py:405
  101.5 1.4 %shard_map.119 = bf16[512,512]{1,0:T(8,128)(2,1)} custom-call(f32[512,512]{1,0:T(8,128)S(1)} %copy-done.6, f32[64,512]{1,0:T(8,128)S(1)} %bitcast.7, bf16[512,512]{1,0:T(8,128)(2,1)S(1)} %copy-done.7, f32[1,512]{1,0:T(1,128)S(1)} %bitcast.11), custom_call_target="tpu_custom_call" | custom-call | flops 2097152 | bytes 2097152 | tf_op jit(solution)/shard_map/pallas_call | solution.py:39
  102.9 2.9 %collective-permute-done.6.refs_3_ = bf16[512,256]{1,0:T(8,128)(2,1)S(1)} collective-permute-done((bf16[512,256]{1,0:T(8,128)(2,1)S(1)}, bf16[512,256]{1,0:T(8,128)(2,1)S(1)}, u32[]{:S(2)}, u32[]{:S(2)}) %collective-permute-start.6) | collective-permute-done | bytes 262176 | tf_op jit(solution)/shard_map/ppermute | solution.py:389
  105.8 2.2 %shard_map.130 = bf16[512,512]{1,0:T(8,128)(2,1)} custom-call(s32[3]{0:T(128)S(1)} %pad_add_fusion.place_ref.refs_0_, s32[256]{0:T(256)S(1)} %copy-done.20, bf16[512,512]{1,0:T(8,128)(2,1)S(1)} %copy-done.19, bf16[512,256]{1,0:T(8,128)(2,1)S(1)} %collective-permute-done.6.refs_3_, f32[4,144,512]{2,1,0:T(8,128)S(1)} %shard_map.129.refs_4_), custom_call_target="tpu_custom_call" | custom-call | flops 4000000000 | bytes 3145728 | tf_op jit(solution)/shard_map/pallas_call | solution.py:405
  (61 shorter events, 12.1 us)
Async XLA Ops:
  0.6 16.2 %copy-start.20 = (s32[256]{0:T(256)S(1)}, s32[256]{0:T(256)}, u32[]{:S(2)}) copy-start(s32[256]{0:T(256)} %refs_1_.9) | copy-start | bytes 3076
  0.6 1.0 copy-start
  5.2 11.6 %copy-start.15 = (bf16[512,512]{1,0:T(8,128)(2,1)S(1)}, bf16[512,512]{1,0:T(8,128)(2,1)}, u32[]{:S(2)}) copy-start(bf16[512,512]{1,0:T(8,128)(2,1)} %refs_2_.9) | copy-start | bytes 1572868
  7.4 20.1 %all-to-all-start = ((bf16[4,144,128]{2,1,0:T(8,128)(2,1)}), bf16[4,144,128]{2,1,0:T(8,128)(2,1)S(1)}, u32[]{:S(2)}, u32[]{:S(2)}) async-start(bf16[4,144,128]{2,1,0:T(8,128)(2,1)} %get-tuple-element.8), calls=%async_computation | async-start | bytes 294912 | tf_op jit(solution)/shard_map/all_to_all | solution.py:247
  13.4 10.0 %collective-permute-start = (bf16[512,256]{1,0:T(8,128)(2,1)}, bf16[512,256]{1,0:T(8,128)(2,1)S(1)}, u32[]{:S(2)}, u32[]{:S(2)}) collective-permute-start(bf16[512,256]{1,0:T(8,128)(2,1)} %get-tuple-element.11.refs_3_), channel_id=1, source_target_pairs={{0,8},{8,16},{16,24},{24,32},{32,40},{40,48},{48,56},{56,64},{64,7... | collective-permute-start | bytes 786440 | tf_op jit(solution)/shard_map/ppermute | solution.py:389
  16.9 4.5 %copy-start.1 = (bf16[512,512]{1,0:T(8,128)(2,1)S(1)}, bf16[512,512]{1,0:T(8,128)(2,1)}, u32[]{:S(2)}) copy-start(bf16[512,512]{1,0:T(8,128)(2,1)} %key_ref.3) | copy-start | bytes 1572868
  16.9 4.5 %copy-start.3 = (bf16[512,512]{1,0:T(8,128)(2,1)S(1)}, bf16[512,512]{1,0:T(8,128)(2,1)}, u32[]{:S(2)}) copy-start(bf16[512,512]{1,0:T(8,128)(2,1)} %value_ref.3) | copy-start | bytes 1572868
  16.9 4.5 %copy-start.4 = (bf16[512,512]{1,0:T(8,128)(2,1)S(1)}, bf16[512,512]{1,0:T(8,128)(2,1)}, u32[]{:S(2)}) copy-start(bf16[512,512]{1,0:T(8,128)(2,1)} %query_ref.3) | copy-start | bytes 1572868
  16.9 4.5 %copy-start.13 = (f32[512,4]{0,1:T(4,128)S(1)}, f32[512,4]{0,1:T(4,128)}, u32[]{:S(2)}) copy-start(f32[512,4]{0,1:T(4,128)} %param.14) | copy-start | bytes 24580
  24.1 15.3 %collective-permute-start.1 = (bf16[512,256]{1,0:T(8,128)(2,1)}, bf16[512,256]{1,0:T(8,128)(2,1)S(1)}, u32[]{:S(2)}, u32[]{:S(2)}) collective-permute-start(bf16[512,256]{1,0:T(8,128)(2,1)} %copy-done.8), channel_id=1, source_target_pairs={{0,8},{8,16},{16,24},{24,32},{32,40},{40,48},{48,56},{56,64},{64,7... | collective-permute-start | bytes 786440 | tf_op jit(solution)/shard_map/ppermute | solution.py:389
  28.2 27.7 %all-to-all-start.1 = ((bf16[4,144,128]{2,1,0:T(8,128)(2,1)}), bf16[4,144,128]{2,1,0:T(8,128)(2,1)S(1)}, u32[]{:S(2)}, u32[]{:S(2)}) async-start(bf16[4,144,128]{2,1,0:T(8,128)(2,1)} %shard_map.115.refs_1_), calls=%async_computation.1 | async-start | bytes 294912 | tf_op jit(solution)/shard_map/all_to_all | solution.py:247
  39.4 13.1 %collective-permute-start.2 = (bf16[512,256]{1,0:T(8,128)(2,1)S(1)}, bf16[512,256]{1,0:T(8,128)(2,1)}, u32[]{:S(2)}, u32[]{:S(2)}) collective-permute-start(bf16[512,256]{1,0:T(8,128)(2,1)S(1)} %shard_map.122.refs_4_), channel_id=1, source_target_pairs={{0,8},{8,16},{16,24},{24,32},{32,40},{40,48},{48,56},{56,64},{64,7... | collective-permute-start | bytes 786440 | tf_op jit(solution)/shard_map/ppermute | solution.py:389
  52.5 8.6 %collective-permute-start.3 = (bf16[512,256]{1,0:T(8,128)(2,1)}, bf16[512,256]{1,0:T(8,128)(2,1)}, u32[]{:S(2)}, u32[]{:S(2)}) collective-permute-start(bf16[512,256]{1,0:T(8,128)(2,1)} %shard_map.124.refs_3_), channel_id=1, source_target_pairs={{0,8},{8,16},{16,24},{24,32},{32,40},{40,48},{48,56},{56,64},{64,7... | collective-permute-start | bytes 786440 | tf_op jit(solution)/shard_map/ppermute | solution.py:389
  56.6 11.1 %all-to-all-start.2 = ((f32[4,136,128]{2,1,0:T(8,128)}), f32[4,136,128]{2,1,0:T(8,128)S(1)}, u32[]{:S(2)}, u32[]{:S(2)}) async-start(f32[4,136,128]{2,1,0:T(8,128)} %shard_map.116.refs_1_), calls=%async_computation.2 | async-start | bytes 557056 | tf_op jit(solution)/shard_map/all_to_all | solution.py:247
  61.1 19.8 %collective-permute-start.4 = (bf16[512,256]{1,0:T(8,128)(2,1)}, bf16[512,256]{1,0:T(8,128)(2,1)}, u32[]{:S(2)}, u32[]{:S(2)}) collective-permute-start(bf16[512,256]{1,0:T(8,128)(2,1)} %shard_map.125.refs_4_), channel_id=1, source_target_pairs={{0,8},{8,16},{16,24},{24,32},{32,40},{40,48},{48,56},{56,64},{64,7... | collective-permute-start | bytes 786440 | tf_op jit(solution)/shard_map/ppermute | solution.py:389
  69.0 18.0 %all-to-all-start.3 = ((bf16[4,128,128]{2,1,0:T(8,128)(2,1)}), bf16[4,128,128]{2,1,0:T(8,128)(2,1)S(1)}, u32[]{:S(2)}, u32[]{:S(2)}) async-start(bf16[4,128,128]{2,1,0:T(8,128)(2,1)} %shard_map.117.refs_1_), calls=%async_computation.3 | async-start | bytes 262144 | tf_op jit(solution)/shard_map/all_to_all | solution.py:247
  81.0 14.4 %collective-permute-start.5 = (bf16[512,256]{1,0:T(8,128)(2,1)}, bf16[512,256]{1,0:T(8,128)(2,1)S(1)}, u32[]{:S(2)}, u32[]{:S(2)}) collective-permute-start(bf16[512,256]{1,0:T(8,128)(2,1)} %shard_map.127.refs_3_), channel_id=1, source_target_pairs={{0,8},{8,16},{16,24},{24,32},{32,40},{40,48},{48,56},{56,64},{64,7... | collective-permute-start | bytes 786440 | tf_op jit(solution)/shard_map/ppermute | solution.py:389
  90.5 11.0 %all-to-all-start.4 = ((f32[8,8,512]{2,1,0:T(8,128)}), f32[8,8,512]{2,1,0:T(8,128)S(1)}, u32[]{:S(2)}, u32[]{:S(2)}) async-start(f32[8,8,512]{2,1,0:T(8,128)} %bitcast.4), calls=%async_computation.4 | async-start | bytes 262144 | tf_op jit(solution)/shard_map/all_to_all | solution.py:522
  95.4 6.1 %copy-start.6 = (f32[512,512]{1,0:T(8,128)S(1)}, f32[512,512]{1,0:T(8,128)}, u32[]{:S(2)}) copy-start(f32[512,512]{1,0:T(8,128)} %copy-done.5) | copy-start | bytes 3145732
  95.4 6.1 %copy-start.7 = (bf16[512,512]{1,0:T(8,128)(2,1)S(1)}, bf16[512,512]{1,0:T(8,128)(2,1)}, u32[]{:S(2)}) copy-start(bf16[512,512]{1,0:T(8,128)(2,1)} %gate_ref.1) | copy-start | bytes 1572868
  95.4 6.1 %copy-start.14 = (f32[512]{0:T(512)S(1)}, f32[512]{0:T(512)}, u32[]{:S(2)}) copy-start(f32[512]{0:T(512)} %param.15) | copy-start | bytes 6148
  95.4 10.4 %collective-permute-start.6 = (bf16[512,256]{1,0:T(8,128)(2,1)S(1)}, bf16[512,256]{1,0:T(8,128)(2,1)S(1)}, u32[]{:S(2)}, u32[]{:S(2)}) collective-permute-start(bf16[512,256]{1,0:T(8,128)(2,1)S(1)} %shard_map.128.refs_4_), channel_id=1, source_target_pairs={{0,8},{8,16},{16,24},{24,32},{32,40},{40,48},{48,56},{56,64},{64,7... | collective-permute-start | bytes 786440 | tf_op jit(solution)/shard_map/ppermute | solution.py:389
  98.9 1.0 copy-start.18
  101.5 4.3 %copy-start.19 = (bf16[512,512]{1,0:T(8,128)(2,1)S(1)}, bf16[512,512]{1,0:T(8,128)(2,1)}, u32[]{:S(2)}) copy-start(bf16[512,512]{1,0:T(8,128)(2,1)} %refs_2_.9) | copy-start | bytes 1572868
  (9 other events, 8.3 us)
where the time goes:
time: 109 us; the launch traced here: 108 us
  starting transfers between devices  59.4 us (54%)
  Pallas kernels  32 us (29%)
  local copies, waits for them, and re-layouts  10.4 us (10%)
  waiting for transfers between devices  5.17 us (5%)
  between operations  1.2 us (1%)
    ppermute x7, starting transfers between devices, forward(): lax.ppermute(array, 'seq', [(s, s + steps) for s in range(shards - steps)])  27.4 us
    all_to_all x4, starting transfers between devices, swap(): lax.all_to_all(array, 'seq', 0, 0, axis_index_groups=groups, tiled=True)  27 us
    pallas_call x5, Pallas kernels, absorb(): pl.pallas_call(functools.partial(attend_body, backs, opening, final), out...  21.3 us
    pallas_call x7, Pallas kernels, call(): pl.pallas_call(body, out_shape=outs, in_specs=specs, out_specs=jax.tree.m...  10.8 us
    unnamed x42, local copies, waits for them, and re-layouts  10.4 us
    all_to_all x1, starting transfers between devices, on_device(): squares = lax.all_to_all(squares, 'head', 0, 0, tiled=True)  4.93 us
    ppermute x7, waiting for transfers between devices, forward(): lax.ppermute(array, 'seq', [(s, s + steps) for s in range(shards - steps)])  3.08 us
  transfers between devices with their start and end apart: 12, of which 3 were waited for; matrix products, arithmetic and copies ran while one was open for 0% of the time, Pallas kernels for 26%

commit v1 on v0

--- a/solution.py
+++ b/solution.py
@@ -23,6 +23,7 @@
 BF16 = jnp.bfloat16
 VMEM_LIMIT = 8 * 1024 * 1024
 ATTEND_LIMIT = 12 * 1024 * 1024
+WHOLE_LIMIT = (64 * 1024 - 512) * 1024
 COST = 4 * 10**9
 
 
@@ -87,9 +88,29 @@
     return packed.astype(BF16)
 
 
-def states_body(key_ref, value_ref, log_ref, soft_key_ref, soft_value_ref, send_ref, first_ref, moving_ref):
-    moving_ref[:, : soft_key_ref.shape[1]] = soft_key_ref[...]
-    moving_ref[:, soft_key_ref.shape[1] :] = soft_value_ref[...]
+def join_body(key_hbm, value_hbm, moving_ref, sems):
+    width = key_hbm.shape[1]
+    copies = [
+        pltpu.make_async_copy(key_hbm, moving_ref.at[:, pl.ds(0, width)], sems.at[0]),
+        pltpu.make_async_copy(value_hbm, moving_ref.at[:, pl.ds(width, width)], sems.at[1]),
+    ]
+    for copy in copies:
+        copy.start()
+    for copy in copies:
+        copy.wait()
+
+
+def states_body(key_hbm, value_hbm, log_hbm, *rest):
+    send_ref, first_ref, key_ref, value_ref, log_ref, sems = rest[-6:]
+    copies = [
+        pltpu.make_async_copy(log_hbm, log_ref, sems.at[0]),
+        pltpu.make_async_copy(key_hbm, key_ref, sems.at[1]),
+        pltpu.make_async_copy(value_hbm, value_ref, sems.at[2]),
+    ]
+    for copy in copies:
+        copy.start()
+    for copy in copies:
+        copy.wait()
     heads = key_ref.shape[1] // HD
     sums = block_sums(log_ref)
     ends = [s[BLK - 1 : BLK, :] for s in sums]
@@ -229,17 +250,41 @@
     tokens, features = lin_key.shape
     heads = features // HD
     logs = log_decay.T
-    send, first, moving = call(
+    anywhere = pl.BlockSpec(memory_space=pl.ANY)
+    vectors = pl.BlockSpec(memory_space=pltpu.VMEM)
+    limit = pltpu.CompilerParams(vmem_limit_bytes=WHOLE_LIMIT)
+    moving = pl.pallas_call(
+        join_body,
+        out_shape=jax.ShapeDtypeStruct((tokens, 2 * soft_key.shape[1]), BF16),
+        in_specs=[anywhere] * 2,
+        out_specs=vectors,
+        scratch_shapes=[pltpu.SemaphoreType.DMA((2,))],
+        compiler_params=limit,
+        cost_estimate=pl.CostEstimate(
+            flops=0, bytes_accessed=8 * soft_key.size, transcendentals=0
+        ),
+    )(soft_key, soft_value)
+    send, first = pl.pallas_call(
         states_body,
-        (
+        out_shape=(
             jax.ShapeDtypeStruct((QUAD, heads * HD // QUAD + LOG_ROWS, HD), BF16),
             jax.ShapeDtypeStruct((heads, HD, HD), F32),
-            jax.ShapeDtypeStruct((tokens, 2 * soft_key.shape[1]), BF16),
         ),
-        (lin_key, lin_value, logs, soft_key, soft_value),
-        flops=4 * tokens * features * HD,
-        moved=4 * tokens * features,
-    )
+        in_specs=[anywhere] * 4,
+        out_specs=(vectors, vectors),
+        scratch_shapes=[
+            pltpu.VMEM((tokens, features), BF16),
+            pltpu.VMEM((tokens, features), BF16),
+            pltpu.VMEM(logs.shape, F32),
+            pltpu.SemaphoreType.DMA((3,)),
+        ],
+        compiler_params=limit,
+        cost_estimate=pl.CostEstimate(
+            flops=4 * tokens * features * HD,
+            bytes_accessed=4 * tokens * features,
+            transcendentals=0,
+        ),
+    )(lin_key, lin_value, logs, moving)
     return logs, send, first, moving
 
 

time: 109 us -> 110 us (level)
  the two profiles are of different devices: /device:TPU:168 before, /device:TPU:72 now
where the time goes in v1:
time: 110 us; the launch traced here: 109 us
  starting transfers between devices  63.2 us (57%)
  Pallas kernels  31.2 us (28%)
  waiting for transfers between devices  8.12 us (7%)
  local copies, waits for them, and re-layouts  5.2 us (5%)
  between operations  1.14 us (1%)
    all_to_all x4, starting transfers between devices, swap(): lax.all_to_all(array, 'seq', 0, 0, axis_index_groups=groups, tiled=True)  29.9 us
    ppermute x7, starting transfers between devices, forward(): lax.ppermute(array, 'seq', [(s, s + steps) for s in range(shards - steps)])  28.4 us
    pallas_call x5, Pallas kernels, absorb(): pl.pallas_call(functools.partial(attend_body, backs, opening, final), out...  17.5 us
    pallas_call x6, Pallas kernels, call(): pl.pallas_call(body, out_shape=outs, in_specs=specs, out_specs=jax.tree.m...  8.64 us
    unnamed x32, local copies, waits for them, and re-layouts  5.2 us
    ppermute x7, waiting for transfers between devices, forward(): lax.ppermute(array, 'seq', [(s, s + steps) for s in range(shards - steps)])  4.86 us
    all_to_all x1, starting transfers between devices, on_device(): squares = lax.all_to_all(squares, 'head', 0, 0, tiled=True)  4.85 us
    pallas_call x1, Pallas kernels, states(): pl.pallas_call(states_body, out_shape=(jax.ShapeDtypeStruct((QUAD, heads...  3.39 us
  transfers between devices with their start and end apart: 12, of which 3 were waited for; matrix products, arithmetic and copies ran while one was open for 0% of the time, Pallas kernels for 25%

profile of v1, /device:TPU:72, one launch (start us, length us, event | category | flops | bytes accessed | tf_op | source)
XLA Modules:
  0.0 109.0 jit_solution(3928921596035118001)
XLA Ops:
  0.6 1.7 %shard_map.113.rest_0_.refs_3_ = bf16[512,256]{1,0:T(8,128)(2,1)} custom-call(bf16[512,128]{1,0:T(8,128)(2,1)} %key_hbm.2, bf16[512,128]{1,0:T(8,128)(2,1)} %value_hbm.2), custom_call_target="tpu_custom_call" | custom-call | bytes 524288 | tf_op jit(solution)/shard_map/pallas_call | solution.py:256
  2.4 4.0 %collective-permute-start = (bf16[512,256]{1,0:T(8,128)(2,1)}, bf16[512,256]{1,0:T(8,128)(2,1)}, u32[]{:S(2)}, u32[]{:S(2)}) collective-permute-start(bf16[512,256]{1,0:T(8,128)(2,1)} %shard_map.113.rest_0_.refs_3_), channel_id=1, source_target_pairs={{0,8},{8,16},{16,24},{24,32},{32,40},{40,48},{48,56},{56,64},{64,7... | collective-permute-start | bytes 786440 | tf_op jit(solution)/shard_map/ppermute | solution.py:434
  6.3 3.4 %shard_map.114 = (bf16[4,144,128]{2,1,0:T(8,128)(2,1)}, f32[4,128,128]{2,1,0:T(8,128)}) custom-call(bf16[512,512]{1,0:T(8,128)(2,1)} %key_ref.1, bf16[512,512]{1,0:T(8,128)(2,1)} %value_ref.1, f32[4,512]{1,0:T(4,128)} %bitcast.8, bf16[512,256]{1,0:T(8,128)(2,1)} %shard_map.113.rest_0_.refs_3_), custom_call_target="tpu_custom_call" | custom-call | flops 134217728 | bytes 1048576 | tf_op jit(solution)/shard_map/pallas_call | solution.py:267
  9.7 6.8 %all-to-all-start = ((bf16[4,144,128]{2,1,0:T(8,128)(2,1)}), bf16[4,144,128]{2,1,0:T(8,128)(2,1)S(1)}, u32[]{:S(2)}, u32[]{:S(2)}) async-start(bf16[4,144,128]{2,1,0:T(8,128)(2,1)} %get-tuple-element.7), calls=%async_computation | async-start | bytes 294912 | tf_op jit(solution)/shard_map/all_to_all | solution.py:292
  17.6 3.9 %shard_map.121.refs_2_.refs_5_ = f32[4,144,512]{2,1,0:T(8,128)S(1)} custom-call(s32[3]{0:T(128)S(1)} %pad_add_fusion.place_ref.refs_0_, s32[256]{0:T(256)S(1)} %copy-done.15, bf16[512,512]{1,0:T(8,128)(2,1)S(1)} %copy-done.10, bf16[512,256]{1,0:T(8,128)(2,1)S(1)} %copy-done.5), custom_call_target="tpu_custom_call" | custom-call | flops 4000000000 | bytes 3145728 | tf_op jit(solution)/shard_map/pallas_call | solution.py:450
  21.6 2.0 %shard_map.115.local_ref.refs_1_ = f32[512,512]{1,0:T(8,128)S(1)} custom-call(bf16[512,512]{1,0:T(8,128)(2,1)S(1)} %copy-done.2, bf16[512,512]{1,0:T(8,128)(2,1)S(1)} %copy-done, bf16[512,512]{1,0:T(8,128)(2,1)S(1)} %copy-done.1, f32[4,512]{1,0:T(4,128)S(1)} %bitcast.9, f32[4,128,128]{2,1,0:T(8,128)S(1)} %copy-done.7), custom_call_target="tpu_custom_call" | custom-call | flops 268435456 | bytes 2621440 | tf_op jit(solution)/shard_map/pallas_call | solution.py:40
  23.6 3.4 %collective-permute-start.1 = (bf16[512,256]{1,0:T(8,128)(2,1)}, bf16[512,256]{1,0:T(8,128)(2,1)S(1)}, u32[]{:S(2)}, u32[]{:S(2)}) collective-permute-start(bf16[512,256]{1,0:T(8,128)(2,1)} %shard_map.122.refs_3_), channel_id=1, source_target_pairs={{0,8},{8,16},{16,24},{24,32},{32,40},{40,48},{48,56},{56,64},{64,7... | collective-permute-start | bytes 786440 | tf_op jit(solution)/shard_map/ppermute | solution.py:434
  27.7 10.4 %all-to-all-start.1 = ((bf16[4,144,128]{2,1,0:T(8,128)(2,1)}), bf16[4,144,128]{2,1,0:T(8,128)(2,1)S(1)}, u32[]{:S(2)}, u32[]{:S(2)}) async-start(bf16[4,144,128]{2,1,0:T(8,128)(2,1)} %shard_map.116.refs_1_), calls=%async_computation.1 | async-start | bytes 294912 | tf_op jit(solution)/shard_map/all_to_all | solution.py:292
  38.1 1.9 %collective-permute-start.2 = (bf16[512,256]{1,0:T(8,128)(2,1)S(1)}, bf16[512,256]{1,0:T(8,128)(2,1)}, u32[]{:S(2)}, u32[]{:S(2)}) collective-permute-start(bf16[512,256]{1,0:T(8,128)(2,1)S(1)} %shard_map.123.refs_4_), channel_id=1, source_target_pairs={{0,8},{8,16},{16,24},{24,32},{32,40},{40,48},{48,56},{56,64},{64,7... | collective-permute-start | bytes 786440 | tf_op jit(solution)/shard_map/ppermute | solution.py:434
  41.1 8.2 %shard_map.124.refs_1_.refs_5_ = f32[4,144,512]{2,1,0:T(8,128)S(1)} custom-call(s32[3]{0:T(128)S(1)} %pad_add_fusion.place_ref.refs_0_, s32[256]{0:T(256)S(1)} %copy-done.15, bf16[512,512]{1,0:T(8,128)(2,1)S(1)} %copy-done.11, bf16[512,256]{1,0:T(8,128)(2,1)} %shard_map.122.refs_3_, ...), custom_call_target="tpu_custom_call", output_to_operand_aliasing={{}: (5, {})} | custom-call | flops 8000000000 | bytes 3145728 | tf_op jit(solution)/shard_map/pallas_call | solution.py:450
  49.2 1.6 %collective-permute-done.2.refs_0_ = bf16[512,256]{1,0:T(8,128)(2,1)} collective-permute-done((bf16[512,256]{1,0:T(8,128)(2,1)S(1)}, bf16[512,256]{1,0:T(8,128)(2,1)}, u32[]{:S(2)}, u32[]{:S(2)}) %collective-permute-start.2) | collective-permute-done | bytes 262176 | tf_op jit(solution)/shard_map/ppermute | solution.py:434
  50.9 5.0 %collective-permute-start.3 = (bf16[512,256]{1,0:T(8,128)(2,1)}, bf16[512,256]{1,0:T(8,128)(2,1)}, u32[]{:S(2)}, u32[]{:S(2)}) collective-permute-start(bf16[512,256]{1,0:T(8,128)(2,1)} %shard_map.125.refs_3_), channel_id=1, source_target_pairs={{0,8},{8,16},{16,24},{24,32},{32,40},{40,48},{48,56},{56,64},{64,7... | collective-permute-start | bytes 786440 | tf_op jit(solution)/shard_map/ppermute | solution.py:434
  56.7 4.3 %all-to-all-start.2 = ((f32[4,136,128]{2,1,0:T(8,128)}), f32[4,136,128]{2,1,0:T(8,128)S(1)}, u32[]{:S(2)}, u32[]{:S(2)}) async-start(f32[4,136,128]{2,1,0:T(8,128)} %shard_map.117.refs_1_), calls=%async_computation.2 | async-start | bytes 557056 | tf_op jit(solution)/shard_map/all_to_all | solution.py:292
  61.0 3.5 %collective-permute-start.4 = (bf16[512,256]{1,0:T(8,128)(2,1)}, bf16[512,256]{1,0:T(8,128)(2,1)}, u32[]{:S(2)}, u32[]{:S(2)}) collective-permute-start(bf16[512,256]{1,0:T(8,128)(2,1)} %shard_map.126.refs_4_), channel_id=1, source_target_pairs={{0,8},{8,16},{16,24},{24,32},{32,40},{40,48},{48,56},{56,64},{64,7... | collective-permute-start | bytes 786440 | tf_op jit(solution)/shard_map/ppermute | solution.py:434
  64.5 3.2 %all-to-all-done.2.wide_ref = f32[4,136,128]{2,1,0:T(8,128)S(1)} async-done(((f32[4,136,128]{2,1,0:T(8,128)}), f32[4,136,128]{2,1,0:T(8,128)S(1)}, u32[]{:S(2)}, u32[]{:S(2)}) %all-to-all-start.2) | async-done | bytes 278560 | tf_op jit(solution)/shard_map/all_to_all | solution.py:292
  69.0 8.5 %all-to-all-start.3 = ((bf16[4,128,128]{2,1,0:T(8,128)(2,1)}), bf16[4,128,128]{2,1,0:T(8,128)(2,1)S(1)}, u32[]{:S(2)}, u32[]{:S(2)}) async-start(bf16[4,128,128]{2,1,0:T(8,128)(2,1)} %shard_map.118.refs_1_), calls=%async_computation.3 | async-start | bytes 262144 | tf_op jit(solution)/shard_map/all_to_all | solution.py:292
  79.9 7.4 %collective-permute-start.5 = (bf16[512,256]{1,0:T(8,128)(2,1)}, bf16[512,256]{1,0:T(8,128)(2,1)S(1)}, u32[]{:S(2)}, u32[]{:S(2)}) collective-permute-start(bf16[512,256]{1,0:T(8,128)(2,1)} %shard_map.128.refs_3_), channel_id=1, source_target_pairs={{0,8},{8,16},{16,24},{24,32},{32,40},{40,48},{48,56},{56,64},{64,7... | collective-permute-start | bytes 786440 | tf_op jit(solution)/shard_map/ppermute | solution.py:434
  87.3 2.5 %shard_map.119 = (f32[512,512]{1,0:T(8,128)S(1)}, f32[64,512]{1,0:T(8,128)}) custom-call(bf16[512,512]{1,0:T(8,128)(2,1)S(1)} %copy-done.2, f32[4,512]{1,0:T(4,128)S(1)} %bitcast.10, f32[512,512]{1,0:T(8,128)S(1)} %shard_map.115.local_ref.refs_1_, bf16[4,128,128]{2,1,0:T(8,128)(2,1)S(1)} %all-to-all-done.3.enter_ref), custom_call_target="tpu_custom_call" | custom-call | flops 67108864 | bytes 2621440 | tf_op jit(solution)/shard_map/pallas_call | solution.py:40
  90.8 4.9 %all-to-all-start.4 = ((f32[8,8,512]{2,1,0:T(8,128)}), f32[8,8,512]{2,1,0:T(8,128)S(1)}, u32[]{:S(2)}, u32[]{:S(2)}) async-start(f32[8,8,512]{2,1,0:T(8,128)} %bitcast.4), calls=%async_computation.4 | async-start | bytes 262144 | tf_op jit(solution)/shard_map/all_to_all | solution.py:567
  95.7 3.3 %collective-permute-start.6 = (bf16[512,256]{1,0:T(8,128)(2,1)S(1)}, bf16[512,256]{1,0:T(8,128)(2,1)}, u32[]{:S(2)}, u32[]{:S(2)}) collective-permute-start(bf16[512,256]{1,0:T(8,128)(2,1)S(1)} %shard_map.129.refs_4_), channel_id=1, source_target_pairs={{0,8},{8,16},{16,24},{24,32},{32,40},{40,48},{48,56},{56,64},{64,7... | collective-permute-start | bytes 786440 | tf_op jit(solution)/shard_map/ppermute | solution.py:434
  100.0 1.5 %shard_map.130.refs_4_ = f32[4,144,512]{2,1,0:T(8,128)S(1)} custom-call(s32[3]{0:T(128)S(1)} %pad_add_fusion.place_ref.refs_0_, s32[256]{0:T(256)S(1)} %copy-done.15, bf16[512,512]{1,0:T(8,128)(2,1)S(1)} %copy-done.13, bf16[512,256]{1,0:T(8,128)(2,1)} %shard_map.128.refs_3_, ...), custom_call_target="tpu_custom_call", output_to_operand_aliasing={{}: (5, {})} | custom-call | flops 8000000000 | bytes 3145728 | tf_op jit(solution)/shard_map/pallas_call | solution.py:450
  101.5 1.4 %shard_map.120 = bf16[512,512]{1,0:T(8,128)(2,1)} custom-call(f32[512,512]{1,0:T(8,128)S(1)} %copy-done.4, f32[64,512]{1,0:T(8,128)S(1)} %bitcast.7, bf16[512,512]{1,0:T(8,128)(2,1)S(1)} %copy-done.6, f32[1,512]{1,0:T(1,128)S(1)} %bitcast.11), custom_call_target="tpu_custom_call" | custom-call | flops 2097152 | bytes 2097152 | tf_op jit(solution)/shard_map/pallas_call | solution.py:40
  102.9 3.2 %collective-permute-done.6.refs_3_ = bf16[512,256]{1,0:T(8,128)(2,1)} collective-permute-done((bf16[512,256]{1,0:T(8,128)(2,1)S(1)}, bf16[512,256]{1,0:T(8,128)(2,1)}, u32[]{:S(2)}, u32[]{:S(2)}) %collective-permute-start.6) | collective-permute-done | bytes 262176 | tf_op jit(solution)/shard_map/ppermute | solution.py:434
  106.2 2.6 %shard_map.131 = bf16[512,512]{1,0:T(8,128)(2,1)} custom-call(s32[3]{0:T(128)S(1)} %pad_add_fusion.place_ref.refs_0_, s32[256]{0:T(256)S(1)} %copy-done.15, bf16[512,512]{1,0:T(8,128)(2,1)S(1)} %copy-done.14, bf16[512,256]{1,0:T(8,128)(2,1)} %collective-permute-done.6.refs_3_, f32[4,144,512]{2,1,0:T(8,128)S(1)} %shard_map.130.refs_4_), custom_call_target="tpu_custom_call" | custom-call | flops 4000000000 | bytes 3145728 | tf_op jit(solution)/shard_map/pallas_call | solution.py:450
  (52 shorter events, 9.4 us)
Async XLA Ops:
  0.6 15.9 %copy-start.15 = (s32[256]{0:T(256)S(1)}, s32[256]{0:T(256)}, u32[]{:S(2)}) copy-start(s32[256]{0:T(256)} %refs_1_.9) | copy-start | bytes 3076
  2.3 14.2 %copy-start.5 = (bf16[512,256]{1,0:T(8,128)(2,1)S(1)}, bf16[512,256]{1,0:T(8,128)(2,1)}, u32[]{:S(2)}) copy-start(bf16[512,256]{1,0:T(8,128)(2,1)} %shard_map.113.rest_0_.refs_3_) | copy-start | bytes 786436
  2.4 21.2 %collective-permute-start = (bf16[512,256]{1,0:T(8,128)(2,1)}, bf16[512,256]{1,0:T(8,128)(2,1)}, u32[]{:S(2)}, u32[]{:S(2)}) collective-permute-start(bf16[512,256]{1,0:T(8,128)(2,1)} %shard_map.113.rest_0_.refs_3_), channel_id=1, source_target_pairs={{0,8},{8,16},{16,24},{24,32},{32,40},{40,48},{48,56},{56,64},{64,7... | collective-permute-start | bytes 786440 | tf_op jit(solution)/shard_map/ppermute | solution.py:434
  9.7 17.3 %all-to-all-start = ((bf16[4,144,128]{2,1,0:T(8,128)(2,1)}), bf16[4,144,128]{2,1,0:T(8,128)(2,1)S(1)}, u32[]{:S(2)}, u32[]{:S(2)}) async-start(bf16[4,144,128]{2,1,0:T(8,128)(2,1)} %get-tuple-element.7), calls=%async_computation | async-start | bytes 294912 | tf_op jit(solution)/shard_map/all_to_all | solution.py:292
  17.6 3.9 %copy-start = (bf16[512,512]{1,0:T(8,128)(2,1)S(1)}, bf16[512,512]{1,0:T(8,128)(2,1)}, u32[]{:S(2)}) copy-start(bf16[512,512]{1,0:T(8,128)(2,1)} %key_ref.1) | copy-start | bytes 1572868
  17.6 3.9 %copy-start.1 = (bf16[512,512]{1,0:T(8,128)(2,1)S(1)}, bf16[512,512]{1,0:T(8,128)(2,1)}, u32[]{:S(2)}) copy-start(bf16[512,512]{1,0:T(8,128)(2,1)} %value_ref.1) | copy-start | bytes 1572868
  17.6 4.0 %copy-start.2 = (bf16[512,512]{1,0:T(8,128)(2,1)S(1)}, bf16[512,512]{1,0:T(8,128)(2,1)}, u32[]{:S(2)}) copy-start(bf16[512,512]{1,0:T(8,128)(2,1)} %query_ref.3) | copy-start | bytes 1572868
  17.6 4.0 %copy-start.7 = (f32[4,128,128]{2,1,0:T(8,128)S(1)}, f32[4,128,128]{2,1,0:T(8,128)}, u32[]{:S(2)}) copy-start(f32[4,128,128]{2,1,0:T(8,128)} %get-tuple-element.6.first_ref) | copy-start | bytes 786436
  17.6 4.0 %copy-start.8 = (f32[512,4]{0,1:T(4,128)S(1)}, f32[512,4]{0,1:T(4,128)}, u32[]{:S(2)}) copy-start(f32[512,4]{0,1:T(4,128)} %param.14) | copy-start | bytes 24580
  23.6 14.5 %collective-permute-start.1 = (bf16[512,256]{1,0:T(8,128)(2,1)}, bf16[512,256]{1,0:T(8,128)(2,1)S(1)}, u32[]{:S(2)}, u32[]{:S(2)}) collective-permute-start(bf16[512,256]{1,0:T(8,128)(2,1)} %shard_map.122.refs_3_), channel_id=1, source_target_pairs={{0,8},{8,16},{16,24},{24,32},{32,40},{40,48},{48,56},{56,64},{64,7... | collective-permute-start | bytes 786440 | tf_op jit(solution)/shard_map/ppermute | solution.py:434
  27.7 28.2 %all-to-all-start.1 = ((bf16[4,144,128]{2,1,0:T(8,128)(2,1)}), bf16[4,144,128]{2,1,0:T(8,128)(2,1)S(1)}, u32[]{:S(2)}, u32[]{:S(2)}) async-start(bf16[4,144,128]{2,1,0:T(8,128)(2,1)} %shard_map.116.refs_1_), calls=%async_computation.1 | async-start | bytes 294912 | tf_op jit(solution)/shard_map/all_to_all | solution.py:292
  38.1 12.8 %collective-permute-start.2 = (bf16[512,256]{1,0:T(8,128)(2,1)S(1)}, bf16[512,256]{1,0:T(8,128)(2,1)}, u32[]{:S(2)}, u32[]{:S(2)}) collective-permute-start(bf16[512,256]{1,0:T(8,128)(2,1)S(1)} %shard_map.123.refs_4_), channel_id=1, source_target_pairs={{0,8},{8,16},{16,24},{24,32},{32,40},{40,48},{48,56},{56,64},{64,7... | collective-permute-start | bytes 786440 | tf_op jit(solution)/shard_map/ppermute | solution.py:434
  50.9 10.1 %collective-permute-start.3 = (bf16[512,256]{1,0:T(8,128)(2,1)}, bf16[512,256]{1,0:T(8,128)(2,1)}, u32[]{:S(2)}, u32[]{:S(2)}) collective-permute-start(bf16[512,256]{1,0:T(8,128)(2,1)} %shard_map.125.refs_3_), channel_id=1, source_target_pairs={{0,8},{8,16},{16,24},{24,32},{32,40},{40,48},{48,56},{56,64},{64,7... | collective-permute-start | bytes 786440 | tf_op jit(solution)/shard_map/ppermute | solution.py:434
  56.7 11.1 %all-to-all-start.2 = ((f32[4,136,128]{2,1,0:T(8,128)}), f32[4,136,128]{2,1,0:T(8,128)S(1)}, u32[]{:S(2)}, u32[]{:S(2)}) async-start(f32[4,136,128]{2,1,0:T(8,128)} %shard_map.117.refs_1_), calls=%async_computation.2 | async-start | bytes 557056 | tf_op jit(solution)/shard_map/all_to_all | solution.py:292
  61.0 18.9 %collective-permute-start.4 = (bf16[512,256]{1,0:T(8,128)(2,1)}, bf16[512,256]{1,0:T(8,128)(2,1)}, u32[]{:S(2)}, u32[]{:S(2)}) collective-permute-start(bf16[512,256]{1,0:T(8,128)(2,1)} %shard_map.126.refs_4_), channel_id=1, source_target_pairs={{0,8},{8,16},{16,24},{24,32},{32,40},{40,48},{48,56},{56,64},{64,7... | collective-permute-start | bytes 786440 | tf_op jit(solution)/shard_map/ppermute | solution.py:434
  69.0 18.3 %all-to-all-start.3 = ((bf16[4,128,128]{2,1,0:T(8,128)(2,1)}), bf16[4,128,128]{2,1,0:T(8,128)(2,1)S(1)}, u32[]{:S(2)}, u32[]{:S(2)}) async-start(bf16[4,128,128]{2,1,0:T(8,128)(2,1)} %shard_map.118.refs_1_), calls=%async_computation.3 | async-start | bytes 262144 | tf_op jit(solution)/shard_map/all_to_all | solution.py:292
  79.9 15.7 %collective-permute-start.5 = (bf16[512,256]{1,0:T(8,128)(2,1)}, bf16[512,256]{1,0:T(8,128)(2,1)S(1)}, u32[]{:S(2)}, u32[]{:S(2)}) collective-permute-start(bf16[512,256]{1,0:T(8,128)(2,1)} %shard_map.128.refs_3_), channel_id=1, source_target_pairs={{0,8},{8,16},{16,24},{24,32},{32,40},{40,48},{48,56},{56,64},{64,7... | collective-permute-start | bytes 786440 | tf_op jit(solution)/shard_map/ppermute | solution.py:434
  90.8 10.7 %all-to-all-start.4 = ((f32[8,8,512]{2,1,0:T(8,128)}), f32[8,8,512]{2,1,0:T(8,128)S(1)}, u32[]{:S(2)}, u32[]{:S(2)}) async-start(f32[8,8,512]{2,1,0:T(8,128)} %bitcast.4), calls=%async_computation.4 | async-start | bytes 262144 | tf_op jit(solution)/shard_map/all_to_all | solution.py:567
  95.6 5.9 %copy-start.4 = (f32[512,512]{1,0:T(8,128)S(1)}, f32[512,512]{1,0:T(8,128)}, u32[]{:S(2)}) copy-start(f32[512,512]{1,0:T(8,128)} %copy-done.3) | copy-start | bytes 3145732
  95.6 5.9 %copy-start.6 = (bf16[512,512]{1,0:T(8,128)(2,1)S(1)}, bf16[512,512]{1,0:T(8,128)(2,1)}, u32[]{:S(2)}) copy-start(bf16[512,512]{1,0:T(8,128)(2,1)} %gate_ref.1) | copy-start | bytes 1572868
  95.6 5.9 %copy-start.9 = (f32[512]{0:T(512)S(1)}, f32[512]{0:T(512)}, u32[]{:S(2)}) copy-start(f32[512]{0:T(512)} %param.15) | copy-start | bytes 6148
  95.7 10.5 %collective-permute-start.6 = (bf16[512,256]{1,0:T(8,128)(2,1)S(1)}, bf16[512,256]{1,0:T(8,128)(2,1)}, u32[]{:S(2)}, u32[]{:S(2)}) collective-permute-start(bf16[512,256]{1,0:T(8,128)(2,1)S(1)} %shard_map.129.refs_4_), channel_id=1, source_target_pairs={{0,8},{8,16},{16,24},{24,32},{32,40},{40,48},{48,56},{56,64},{64,7... | collective-permute-start | bytes 786440 | tf_op jit(solution)/shard_map/ppermute | solution.py:434
  98.9 1.0 copy-start.13
  101.5 4.7 %copy-start.14 = (bf16[512,512]{1,0:T(8,128)(2,1)S(1)}, bf16[512,512]{1,0:T(8,128)(2,1)}, u32[]{:S(2)}) copy-start(bf16[512,512]{1,0:T(8,128)(2,1)} %refs_2_.9) | copy-start | bytes 1572868
  (4 other events, 4.1 us)

commit v2 on v1

--- a/solution.py
+++ b/solution.py
@@ -23,6 +23,7 @@
 BF16 = jnp.bfloat16
 VMEM_LIMIT = 8 * 1024 * 1024
 ATTEND_LIMIT = 12 * 1024 * 1024
+NEARLY_ALL = (64 * 1024 - 768) * 1024
 WHOLE_LIMIT = (64 * 1024 - 512) * 1024
 COST = 4 * 10**9
 
@@ -317,7 +318,10 @@
     pieces = refs[3 : 3 + len(backs)]
     rest = refs[3 + len(backs) :]
     acc_hbm = None if opening else rest[0]
-    out_ref, query_ref, acc_ref, query_sem, in_sem, out_sem = rest[-6:]
+    query_ref, acc_ref, query_sem, in_sem, out_sem = rest[-5:]
+    out_ref = rest[-6] if final else rest[-7]
+    if not final:
+        rest[-6][...] = jnp.zeros_like(rest[-6])
     tokens, features = query_hbm.shape
     heads = features // HD
     blocks = tokens // MBLK
@@ -440,6 +444,7 @@
     heads = features // HD
     rows = heads * MBLK
     carry = jax.ShapeDtypeStruct((blocks, HD + 16, rows), F32)
+    mark = jax.ShapeDtypeStruct((8, HD), F32)
     anywhere = pl.BlockSpec(memory_space=pl.ANY)
     scalars = pl.BlockSpec(memory_space=pltpu.SMEM)
     vectors = pl.BlockSpec(memory_space=pltpu.VMEM)
@@ -449,12 +454,12 @@
         held = [] if opening else [state]
         return pl.pallas_call(
             functools.partial(attend_body, backs, opening, final),
-            out_shape=jax.ShapeDtypeStruct((tokens, features), BF16) if final else carry,
+            out_shape=jax.ShapeDtypeStruct((tokens, features), BF16) if final else (carry, mark),
             in_specs=[scalars] * 2
             + [anywhere]
             + [vectors] * len(backs)
             + [anywhere] * len(held),
-            out_specs=vectors if final else anywhere,
+            out_specs=vectors if final else (anywhere, vectors),
             scratch_shapes=[
                 pltpu.VMEM((blocks, MBLK, features), BF16),
                 pltpu.VMEM(carry.shape, F32),
@@ -463,7 +468,7 @@
                 pltpu.SemaphoreType.DMA((blocks,)),
             ],
             input_output_aliases={3 + len(backs): 0} if held and not final else {},
-            compiler_params=pltpu.CompilerParams(vmem_limit_bytes=ATTEND_LIMIT),
+            compiler_params=pltpu.CompilerParams(vmem_limit_bytes=ATTEND_LIMIT if final else NEARLY_ALL),
             cost_estimate=pl.CostEstimate(
                 flops=len(backs) * COST,
                 bytes_accessed=12 * tokens * features,
@@ -522,8 +527,8 @@
         flops=4 * tokens * features * BLK,
         moved=10 * tokens * features,
     )
-    state = absorb(None, (0,), back[:1])
-    hop(local, state)
+    state, mark = absorb(None, (0,), back[:1])
+    hop(local, mark)
     group = call(
         group_body,
         jax.ShapeDtypeStruct((QUAD, size + LOG_ROWS, HD), BF16),
@@ -532,8 +537,8 @@
     )
     lines = swap(group, line)
     hop(group)
-    state = absorb(state, (1, 2), back[1:3])
-    hop(state)
+    state, mark = absorb(state, (1, 2), back[1:3])
+    hop(mark)
     total = call(
         group_body,
         jax.ShapeDtypeStruct((shards // span, size + 8, HD), F32),
@@ -542,8 +547,8 @@
     )
     wides = swap(total, wide)
     hop(total)
-    state = absorb(state, (3, 4), back[3:5])
-    hop(state)
+    state, mark = absorb(state, (3, 4), back[3:5])
+    hop(mark)
     entering = call(
         enter_body,
         jax.ShapeDtypeStruct((QUAD, size, HD), BF16),
@@ -553,7 +558,7 @@
     )
     hop(entering)
     entering = swap(entering, near).reshape(heads, HD, HD)
-    state = absorb(state, (5, 6), back[5:7])
+    state, mark = absorb(state, (5, 6), back[5:7])
     raw, squares = call(
         raw_body,
         (

time: 110 us -> 119 us (1.082)
  the two profiles are of different devices: /device:TPU:72 before, /device:TPU:10 now
where the time goes in v2:
time: 119 us
  starting transfers between devices  51.3 us (43%)
  Pallas kernels  42.6 us (36%)
  waiting for transfers between devices  14.6 us (12%)
  local copies, waits for them, and re-layouts  8.85 us (7%)
    pallas_call x5, Pallas kernels, absorb(): pl.pallas_call(functools.partial(attend_body, backs, opening, final), out...  28.9 us
    all_to_all x4, starting transfers between devices, swap(): lax.all_to_all(array, 'seq', 0, 0, axis_index_groups=groups, tiled=True)  25.7 us
    ppermute x7, starting transfers between devices, forward(): lax.ppermute(array, 'seq', [(s, s + steps) for s in range(shards - steps)])  20.7 us
    ppermute x7, waiting for transfers between devices, forward(): lax.ppermute(array, 'seq', [(s, s + steps) for s in range(shards - steps)])  14.1 us
    unnamed x42, local copies, waits for them, and re-layouts  8.85 us
    pallas_call x6, Pallas kernels, call(): pl.pallas_call(body, out_shape=outs, in_specs=specs, out_specs=jax.tree.m...  8.63 us
    all_to_all x1, starting transfers between devices, on_device(): squares = lax.all_to_all(squares, 'head', 0, 0, tiled=True)  4.88 us
    pallas_call x1, Pallas kernels, states(): pl.pallas_call(states_body, out_shape=(jax.ShapeDtypeStruct((QUAD, heads...  3.38 us
  transfers between devices with their start and end apart: 12, of which 4 were waited for; matrix products, arithmetic and copies ran while one was open for 1% of the time, Pallas kernels for 32%

profile of v2, /device:TPU:10, one launch (start us, length us, event | category | flops | bytes accessed | tf_op | source)
XLA Modules:
  0.0 119.1 jit_solution(9964293440230532870)
XLA Ops:
  0.6 1.7 %shard_map.113.rest_0_.refs_3_ = bf16[512,256]{1,0:T(8,128)(2,1)} custom-call(bf16[512,128]{1,0:T(8,128)(2,1)} %key_hbm.2, bf16[512,128]{1,0:T(8,128)(2,1)} %value_hbm.2), custom_call_target="tpu_custom_call" | custom-call | bytes 524288 | tf_op jit(solution)/shard_map/pallas_call | solution.py:257
  2.3 3.8 %collective-permute-start = (bf16[512,256]{1,0:T(8,128)(2,1)}, bf16[512,256]{1,0:T(8,128)(2,1)}, u32[]{:S(2)}, u32[]{:S(2)}) collective-permute-start(bf16[512,256]{1,0:T(8,128)(2,1)} %shard_map.113.rest_0_.refs_3_), channel_id=1, source_target_pairs={{0,8},{8,16},{16,24},{24,32},{32,40},{40,48},{48,56},{56,64},{64,7... | collective-permute-start | bytes 786440 | tf_op jit(solution)/shard_map/ppermute | solution.py:438
  6.2 3.4 %shard_map.114 = (bf16[4,144,128]{2,1,0:T(8,128)(2,1)}, f32[4,128,128]{2,1,0:T(8,128)}) custom-call(bf16[512,512]{1,0:T(8,128)(2,1)} %key_ref.1, bf16[512,512]{1,0:T(8,128)(2,1)} %value_ref.1, f32[4,512]{1,0:T(4,128)} %bitcast.8, bf16[512,256]{1,0:T(8,128)(2,1)} %shard_map.113.rest_0_.refs_3_), custom_call_target="tpu_custom_call" | custom-call | flops 134217728 | bytes 1048576 | tf_op jit(solution)/shard_map/pallas_call | solution.py:268
  9.6 7.1 %all-to-all-start = ((bf16[4,144,128]{2,1,0:T(8,128)(2,1)}), bf16[4,144,128]{2,1,0:T(8,128)(2,1)S(1)}, u32[]{:S(2)}, u32[]{:S(2)}) async-start(bf16[4,144,128]{2,1,0:T(8,128)(2,1)} %get-tuple-element.14), calls=%async_computation | async-start | bytes 294912 | tf_op jit(solution)/shard_map/all_to_all | solution.py:293
  17.3 5.7 %shard_map.121 = (f32[4,144,512]{2,1,0:T(8,128)}, f32[8,128]{1,0:T(8,128)}) custom-call(s32[3]{0:T(128)} %pad_add_fusion.place_ref.refs_0_, s32[256]{0:T(256)} %refs_1_.9, bf16[512,512]{1,0:T(8,128)(2,1)} %refs_2_.9, bf16[512,256]{1,0:T(8,128)(2,1)} %shard_map.113.rest_0_.refs_3_), custom_call_target="tpu_custom_call" | custom-call | flops 4000000000 | bytes 3145728 | tf_op jit(solution)/shard_map/pallas_call | solution.py:455
  26.0 2.0 %shard_map.115.local_ref.refs_1_ = f32[512,512]{1,0:T(8,128)S(1)} custom-call(bf16[512,512]{1,0:T(8,128)(2,1)S(1)} %copy-done.4, bf16[512,512]{1,0:T(8,128)(2,1)S(1)} %copy-done.2, bf16[512,512]{1,0:T(8,128)(2,1)S(1)} %copy-done.3, f32[4,512]{1,0:T(4,128)S(1)} %bitcast.9, f32[4,128,128]{2,1,0:T(8,128)S(1)} %copy-done.10), custom_call_target="tpu_custom_call" | custom-call | flops 268435456 | bytes 2621440 | tf_op jit(solution)/shard_map/pallas_call | solution.py:41
  29.1 3.9 %collective-permute-start.1 = (bf16[512,256]{1,0:T(8,128)(2,1)}, bf16[512,256]{1,0:T(8,128)(2,1)S(1)}, u32[]{:S(2)}, u32[]{:S(2)}) collective-permute-start(bf16[512,256]{1,0:T(8,128)(2,1)} %shard_map.122.refs_3_), channel_id=1, source_target_pairs={{0,8},{8,16},{16,24},{24,32},{32,40},{40,48},{48,56},{56,64},{64,7... | collective-permute-start | bytes 786440 | tf_op jit(solution)/shard_map/ppermute | solution.py:438
  33.7 10.4 %all-to-all-start.1 = ((bf16[4,144,128]{2,1,0:T(8,128)(2,1)}), bf16[4,144,128]{2,1,0:T(8,128)(2,1)S(1)}, u32[]{:S(2)}, u32[]{:S(2)}) async-start(bf16[4,144,128]{2,1,0:T(8,128)(2,1)} %shard_map.116.refs_1_), calls=%async_computation.1 | async-start | bytes 294912 | tf_op jit(solution)/shard_map/all_to_all | solution.py:293
  44.1 3.4 %collective-permute-start.2 = (bf16[512,256]{1,0:T(8,128)(2,1)S(1)}, bf16[512,256]{1,0:T(8,128)(2,1)}, u32[]{:S(2)}, u32[]{:S(2)}) collective-permute-start(bf16[512,256]{1,0:T(8,128)(2,1)S(1)} %shard_map.123.refs_4_), channel_id=1, source_target_pairs={{0,8},{8,16},{16,24},{24,32},{32,40},{40,48},{48,56},{56,64},{64,7... | collective-permute-start | bytes 786440 | tf_op jit(solution)/shard_map/ppermute | solution.py:438
  47.5 9.2 %shard_map.124 = (f32[4,144,512]{2,1,0:T(8,128)}, f32[8,128]{1,0:T(8,128)}) custom-call(s32[3]{0:T(128)} %pad_add_fusion.place_ref.refs_0_, s32[256]{0:T(256)} %refs_1_.9, bf16[512,512]{1,0:T(8,128)(2,1)} %refs_2_.9, bf16[512,256]{1,0:T(8,128)(2,1)} %shard_map.122.refs_3_, bf16[512,256]{1,0:T(8,128)(2,1)} %copy-done.9, ...), custom_call_target="tpu_custom_call", output_to_operand_aliasing={{0}: (5, {})} | custom-call | flops 8000000000 | bytes 3145728 | tf_op jit(solution)/shard_map/pallas_call | solution.py:455
  56.7 4.3 %collective-permute-done.2.refs_0_ = bf16[512,256]{1,0:T(8,128)(2,1)} collective-permute-done((bf16[512,256]{1,0:T(8,128)(2,1)S(1)}, bf16[512,256]{1,0:T(8,128)(2,1)}, u32[]{:S(2)}, u32[]{:S(2)}) %collective-permute-start.2) | collective-permute-done | bytes 262176 | tf_op jit(solution)/shard_map/ppermute | solution.py:438
  61.7 1.9 %collective-permute-start.3 = (bf16[512,256]{1,0:T(8,128)(2,1)}, bf16[512,256]{1,0:T(8,128)(2,1)}, u32[]{:S(2)}, u32[]{:S(2)}) collective-permute-start(bf16[512,256]{1,0:T(8,128)(2,1)} %shard_map.125.refs_3_), channel_id=1, source_target_pairs={{0,8},{8,16},{16,24},{24,32},{32,40},{40,48},{48,56},{56,64},{64,7... | collective-permute-start | bytes 786440 | tf_op jit(solution)/shard_map/ppermute | solution.py:438
  64.4 4.9 %all-to-all-start.2 = ((f32[4,136,128]{2,1,0:T(8,128)}), f32[4,136,128]{2,1,0:T(8,128)S(1)}, u32[]{:S(2)}, u32[]{:S(2)}) async-start(f32[4,136,128]{2,1,0:T(8,128)} %shard_map.117.refs_1_), calls=%async_computation.2 | async-start | bytes 557056 | tf_op jit(solution)/shard_map/all_to_all | solution.py:293
  69.3 4.4 %collective-permute-done.3.refs_0_ = bf16[512,256]{1,0:T(8,128)(2,1)} collective-permute-done((bf16[512,256]{1,0:T(8,128)(2,1)}, bf16[512,256]{1,0:T(8,128)(2,1)}, u32[]{:S(2)}, u32[]{:S(2)}) %collective-permute-start.3) | collective-permute-done | bytes 262176 | tf_op jit(solution)/shard_map/ppermute | solution.py:438
  73.8 1.9 %collective-permute-start.4 = (bf16[512,256]{1,0:T(8,128)(2,1)}, bf16[512,256]{1,0:T(8,128)(2,1)}, u32[]{:S(2)}, u32[]{:S(2)}) collective-permute-start(bf16[512,256]{1,0:T(8,128)(2,1)} %shard_map.126.refs_4_), channel_id=1, source_target_pairs={{0,8},{8,16},{16,24},{24,32},{32,40},{40,48},{48,56},{56,64},{64,7... | collective-permute-start | bytes 786440 | tf_op jit(solution)/shard_map/ppermute | solution.py:438
  77.0 3.3 %all-to-all-start.3 = ((bf16[4,128,128]{2,1,0:T(8,128)(2,1)}), bf16[4,128,128]{2,1,0:T(8,128)(2,1)S(1)}, u32[]{:S(2)}, u32[]{:S(2)}) async-start(bf16[4,128,128]{2,1,0:T(8,128)(2,1)} %shard_map.118.refs_1_), calls=%async_computation.3 | async-start | bytes 262144 | tf_op jit(solution)/shard_map/all_to_all | solution.py:293
  80.3 9.1 %shard_map.127 = (f32[4,144,512]{2,1,0:T(8,128)}, f32[8,128]{1,0:T(8,128)}) custom-call(s32[3]{0:T(128)} %pad_add_fusion.place_ref.refs_0_, s32[256]{0:T(256)} %refs_1_.9, bf16[512,512]{1,0:T(8,128)(2,1)} %refs_2_.9, bf16[512,256]{1,0:T(8,128)(2,1)} %shard_map.125.refs_3_, bf16[512,256]{1,0:T(8,128)(2,1)} %shard_map.126.refs_4_, ...), custom_call_target="tpu_custom_call", output_to_operand_aliasing={{0}: (5, {})} | custom-call | flops 8000000000 | bytes 3145728 | tf_op jit(solution)/shard_map/pallas_call | solution.py:455
  90.2 3.9 %collective-permute-start.5 = (bf16[512,256]{1,0:T(8,128)(2,1)}, bf16[512,256]{1,0:T(8,128)(2,1)}, u32[]{:S(2)}, u32[]{:S(2)}) collective-permute-start(bf16[512,256]{1,0:T(8,128)(2,1)} %shard_map.128.refs_3_), channel_id=1, source_target_pairs={{0,8},{8,16},{16,24},{24,32},{32,40},{40,48},{48,56},{56,64},{64,7... | collective-permute-start | bytes 786440 | tf_op jit(solution)/shard_map/ppermute | solution.py:438
  95.3 2.5 %shard_map.119 = (f32[512,512]{1,0:T(8,128)S(1)}, f32[64,512]{1,0:T(8,128)}) custom-call(bf16[512,512]{1,0:T(8,128)(2,1)S(1)} %copy-done.5, f32[4,512]{1,0:T(4,128)S(1)} %bitcast.10, f32[512,512]{1,0:T(8,128)S(1)} %copy-done.1, bf16[4,128,128]{2,1,0:T(8,128)(2,1)S(1)} %all-to-all-done.3.enter_ref), custom_call_target="tpu_custom_call" | custom-call | flops 67108864 | bytes 2621440 | tf_op jit(solution)/shard_map/pallas_call | solution.py:41
  98.7 4.9 %all-to-all-start.4 = ((f32[8,8,512]{2,1,0:T(8,128)}), f32[8,8,512]{2,1,0:T(8,128)S(1)}, u32[]{:S(2)}, u32[]{:S(2)}) async-start(f32[8,8,512]{2,1,0:T(8,128)} %bitcast.4), calls=%async_computation.4 | async-start | bytes 262144 | tf_op jit(solution)/shard_map/all_to_all | solution.py:572
  103.6 1.9 %collective-permute-start.6 = (bf16[512,256]{1,0:T(8,128)(2,1)}, bf16[512,256]{1,0:T(8,128)(2,1)}, u32[]{:S(2)}, u32[]{:S(2)}) collective-permute-start(bf16[512,256]{1,0:T(8,128)(2,1)} %shard_map.129.refs_4_), channel_id=1, source_target_pairs={{0,8},{8,16},{16,24},{24,32},{32,40},{40,48},{48,56},{56,64},{64,7... | collective-permute-start | bytes 786440 | tf_op jit(solution)/shard_map/ppermute | solution.py:438
  105.6 2.2 %shard_map.130 = (f32[4,144,512]{2,1,0:T(8,128)}, f32[8,128]{1,0:T(8,128)}) custom-call(s32[3]{0:T(128)} %pad_add_fusion.place_ref.refs_0_, s32[256]{0:T(256)} %refs_1_.9, bf16[512,512]{1,0:T(8,128)(2,1)} %refs_2_.9, bf16[512,256]{1,0:T(8,128)(2,1)} %shard_map.128.refs_3_, bf16[512,256]{1,0:T(8,128)(2,1)} %shard_map.129.refs_4_, ...), custom_call_target="tpu_custom_call", output_to_operand_aliasing={{0}: (5, {})} | custom-call | flops 8000000000 | bytes 3145728 | tf_op jit(solution)/shard_map/pallas_call | solution.py:455
  110.9 5.3 %collective-permute-done.6.refs_3_ = bf16[512,256]{1,0:T(8,128)(2,1)} collective-permute-done((bf16[512,256]{1,0:T(8,128)(2,1)}, bf16[512,256]{1,0:T(8,128)(2,1)}, u32[]{:S(2)}, u32[]{:S(2)}) %collective-permute-start.6) | collective-permute-done | bytes 262176 | tf_op jit(solution)/shard_map/ppermute | solution.py:438
  116.3 2.6 %shard_map.131 = bf16[512,512]{1,0:T(8,128)(2,1)} custom-call(s32[3]{0:T(128)S(1)} %copy-done.17, s32[256]{0:T(256)S(1)} %copy-done.19, bf16[512,512]{1,0:T(8,128)(2,1)S(1)} %copy-done.18, bf16[512,256]{1,0:T(8,128)(2,1)} %collective-permute-done.6.refs_3_, f32[4,144,512]{2,1,0:T(8,128)S(1)} %copy-done.20), custom_call_target="tpu_custom_call" | custom-call | flops 4000000000 | bytes 3145728 | tf_op jit(solution)/shard_map/pallas_call | solution.py:455
  (62 shorter events, 14.2 us)
Async XLA Ops:
  2.3 25.7 %collective-permute-start = (bf16[512,256]{1,0:T(8,128)(2,1)}, bf16[512,256]{1,0:T(8,128)(2,1)}, u32[]{:S(2)}, u32[]{:S(2)}) collective-permute-start(bf16[512,256]{1,0:T(8,128)(2,1)} %shard_map.113.rest_0_.refs_3_), channel_id=1, source_target_pairs={{0,8},{8,16},{16,24},{24,32},{32,40},{40,48},{48,56},{56,64},{64,7... | collective-permute-start | bytes 786440 | tf_op jit(solution)/shard_map/ppermute | solution.py:438
  9.6 23.5 %all-to-all-start = ((bf16[4,144,128]{2,1,0:T(8,128)(2,1)}), bf16[4,144,128]{2,1,0:T(8,128)(2,1)S(1)}, u32[]{:S(2)}, u32[]{:S(2)}) async-start(bf16[4,144,128]{2,1,0:T(8,128)(2,1)} %get-tuple-element.14), calls=%async_computation | async-start | bytes 294912 | tf_op jit(solution)/shard_map/all_to_all | solution.py:293
  17.3 5.7 %copy-start.2 = (bf16[512,512]{1,0:T(8,128)(2,1)S(1)}, bf16[512,512]{1,0:T(8,128)(2,1)}, u32[]{:S(2)}) copy-start(bf16[512,512]{1,0:T(8,128)(2,1)} %key_ref.1) | copy-start | bytes 1572868
  17.3 5.7 %copy-start.11 = (f32[512,4]{0,1:T(4,128)S(1)}, f32[512,4]{0,1:T(4,128)}, u32[]{:S(2)}) copy-start(f32[512,4]{0,1:T(4,128)} %param.14) | copy-start | bytes 24580
  26.0 2.0 %copy-start.12 = (f32[8,128]{1,0:T(8,128)S(1)}, f32[8,128]{1,0:T(8,128)}, u32[]{:S(2)}) copy-start(f32[8,128]{1,0:T(8,128)} %get-tuple-element.17.refs_2_) | copy-start | bytes 12292
  29.1 15.0 %collective-permute-start.1 = (bf16[512,256]{1,0:T(8,128)(2,1)}, bf16[512,256]{1,0:T(8,128)(2,1)S(1)}, u32[]{:S(2)}, u32[]{:S(2)}) collective-permute-start(bf16[512,256]{1,0:T(8,128)(2,1)} %shard_map.122.refs_3_), channel_id=1, source_target_pairs={{0,8},{8,16},{16,24},{24,32},{32,40},{40,48},{48,56},{56,64},{64,7... | collective-permute-start | bytes 786440 | tf_op jit(solution)/shard_map/ppermute | solution.py:438
  33.7 29.9 %all-to-all-start.1 = ((bf16[4,144,128]{2,1,0:T(8,128)(2,1)}), bf16[4,144,128]{2,1,0:T(8,128)(2,1)S(1)}, u32[]{:S(2)}, u32[]{:S(2)}) async-start(bf16[4,144,128]{2,1,0:T(8,128)(2,1)} %shard_map.116.refs_1_), calls=%async_computation.1 | async-start | bytes 294912 | tf_op jit(solution)/shard_map/all_to_all | solution.py:293
  44.1 3.4 %copy-start.9 = (bf16[512,256]{1,0:T(8,128)(2,1)}, bf16[512,256]{1,0:T(8,128)(2,1)S(1)}, u32[]{:S(2)}) copy-start(bf16[512,256]{1,0:T(8,128)(2,1)S(1)} %shard_map.123.refs_4_) | copy-start | bytes 786436
  44.1 16.9 %collective-permute-start.2 = (bf16[512,256]{1,0:T(8,128)(2,1)S(1)}, bf16[512,256]{1,0:T(8,128)(2,1)}, u32[]{:S(2)}, u32[]{:S(2)}) collective-permute-start(bf16[512,256]{1,0:T(8,128)(2,1)S(1)} %shard_map.123.refs_4_), channel_id=1, source_target_pairs={{0,8},{8,16},{16,24},{24,32},{32,40},{40,48},{48,56},{56,64},{64,7... | collective-permute-start | bytes 786440 | tf_op jit(solution)/shard_map/ppermute | solution.py:438
  56.7 18.9 %copy-start.16 = (s32[3]{0:T(128)S(1)}, s32[3]{0:T(128)}, u32[]{:S(2)}) copy-start(s32[3]{0:T(128)} %pad_add_fusion.place_ref.refs_0_) | copy-start | bytes 40
  61.7 12.0 %collective-permute-start.3 = (bf16[512,256]{1,0:T(8,128)(2,1)}, bf16[512,256]{1,0:T(8,128)(2,1)}, u32[]{:S(2)}, u32[]{:S(2)}) collective-permute-start(bf16[512,256]{1,0:T(8,128)(2,1)} %shard_map.125.refs_3_), channel_id=1, source_target_pairs={{0,8},{8,16},{16,24},{24,32},{32,40},{40,48},{48,56},{56,64},{64,7... | collective-permute-start | bytes 786440 | tf_op jit(solution)/shard_map/ppermute | solution.py:438
  64.4 11.3 %all-to-all-start.2 = ((f32[4,136,128]{2,1,0:T(8,128)}), f32[4,136,128]{2,1,0:T(8,128)S(1)}, u32[]{:S(2)}, u32[]{:S(2)}) async-start(f32[4,136,128]{2,1,0:T(8,128)} %shard_map.117.refs_1_), calls=%async_computation.2 | async-start | bytes 557056 | tf_op jit(solution)/shard_map/all_to_all | solution.py:293
  73.8 15.7 %collective-permute-start.4 = (bf16[512,256]{1,0:T(8,128)(2,1)}, bf16[512,256]{1,0:T(8,128)(2,1)}, u32[]{:S(2)}, u32[]{:S(2)}) collective-permute-start(bf16[512,256]{1,0:T(8,128)(2,1)} %shard_map.126.refs_4_), channel_id=1, source_target_pairs={{0,8},{8,16},{16,24},{24,32},{32,40},{40,48},{48,56},{56,64},{64,7... | collective-permute-start | bytes 786440 | tf_op jit(solution)/shard_map/ppermute | solution.py:438
  77.0 17.1 %all-to-all-start.3 = ((bf16[4,128,128]{2,1,0:T(8,128)(2,1)}), bf16[4,128,128]{2,1,0:T(8,128)(2,1)S(1)}, u32[]{:S(2)}, u32[]{:S(2)}) async-start(bf16[4,128,128]{2,1,0:T(8,128)(2,1)} %shard_map.118.refs_1_), calls=%async_computation.3 | async-start | bytes 262144 | tf_op jit(solution)/shard_map/all_to_all | solution.py:293
  80.3 13.7 %copy-start.5 = (bf16[512,512]{1,0:T(8,128)(2,1)S(1)}, bf16[512,512]{1,0:T(8,128)(2,1)}, u32[]{:S(2)}) copy-start(bf16[512,512]{1,0:T(8,128)(2,1)} %query_ref.3) | copy-start | bytes 1572868
  90.2 13.4 %collective-permute-start.5 = (bf16[512,256]{1,0:T(8,128)(2,1)}, bf16[512,256]{1,0:T(8,128)(2,1)}, u32[]{:S(2)}, u32[]{:S(2)}) collective-permute-start(bf16[512,256]{1,0:T(8,128)(2,1)} %shard_map.128.refs_3_), channel_id=1, source_target_pairs={{0,8},{8,16},{16,24},{24,32},{32,40},{40,48},{48,56},{56,64},{64,7... | collective-permute-start | bytes 786440 | tf_op jit(solution)/shard_map/ppermute | solution.py:438
  98.7 9.6 %all-to-all-start.4 = ((f32[8,8,512]{2,1,0:T(8,128)}), f32[8,8,512]{2,1,0:T(8,128)S(1)}, u32[]{:S(2)}, u32[]{:S(2)}) async-start(f32[8,8,512]{2,1,0:T(8,128)} %bitcast.4), calls=%async_computation.4 | async-start | bytes 262144 | tf_op jit(solution)/shard_map/all_to_all | solution.py:572
  103.6 12.7 %collective-permute-start.6 = (bf16[512,256]{1,0:T(8,128)(2,1)}, bf16[512,256]{1,0:T(8,128)(2,1)}, u32[]{:S(2)}, u32[]{:S(2)}) collective-permute-start(bf16[512,256]{1,0:T(8,128)(2,1)} %shard_map.129.refs_4_), channel_id=1, source_target_pairs={{0,8},{8,16},{16,24},{24,32},{32,40},{40,48},{48,56},{56,64},{64,7... | collective-permute-start | bytes 786440 | tf_op jit(solution)/shard_map/ppermute | solution.py:438
  105.5 2.8 %copy-start.8 = (bf16[512,512]{1,0:T(8,128)(2,1)S(1)}, bf16[512,512]{1,0:T(8,128)(2,1)}, u32[]{:S(2)}) copy-start(bf16[512,512]{1,0:T(8,128)(2,1)} %gate_ref.1) | copy-start | bytes 1572868
  105.5 2.7 %copy-start.15 = (f32[512]{0:T(512)S(1)}, f32[512]{0:T(512)}, u32[]{:S(2)}) copy-start(f32[512]{0:T(512)} %param.15) | copy-start | bytes 6148
  107.8 8.5 %copy-start.17 = (s32[3]{0:T(128)S(1)}, s32[3]{0:T(128)}, u32[]{:S(2)}) copy-start(s32[3]{0:T(128)} %pad_add_fusion.place_ref.refs_0_) | copy-start | bytes 40
  107.8 8.5 %copy-start.19 = (s32[256]{0:T(256)S(1)}, s32[256]{0:T(256)}, u32[]{:S(2)}) copy-start(s32[256]{0:T(256)} %refs_1_.9) | copy-start | bytes 3076
  109.5 6.8 %copy-start.18 = (bf16[512,512]{1,0:T(8,128)(2,1)S(1)}, bf16[512,512]{1,0:T(8,128)(2,1)}, u32[]{:S(2)}) copy-start(bf16[512,512]{1,0:T(8,128)(2,1)} %refs_2_.9) | copy-start | bytes 1572868
  109.5 6.8 %copy-start.20 = (f32[4,144,512]{2,1,0:T(8,128)S(1)}, f32[4,144,512]{2,1,0:T(8,128)}, u32[]{:S(2)}) copy-start(f32[4,144,512]{2,1,0:T(8,128)} %get-tuple-element.23.refs_4_) | copy-start | bytes 3538948
  (9 other events, 8.8 us)
